TPU v7x, 32 devices: a whole 2x2x4 slice. The times are simulated.
32 devices in a mesh: pts: 4 (over x, core), snap: 8 (over z, y).
Axes of the slice: x: 2, y: 2, z: 4, core: 2. Of those that a mesh axis runs over, the one named last changes fastest.
Arguments:
- snapshots: float32 [4096, 8192], P('pts', 'snap'), may hold values from -8 to 8
- modes_init: float32 [4096, 128], P('pts'), may hold values from -6 to 6
- coefs_init: float32 [128, 8192], P(None, 'snap'), may hold values from -0.09375 to 0.09375
Outputs:
- modes: float32 [4096, 128], P('pts')
- amplitudes: float32 [128, 8192], P(None, 'snap')
All inputs are finite; a program needn't handle non-finite values.
Results may differ from a plain program's by a relative error of at most 0.0003.
Values sent between devices are 32-bit elements; how exact they have to be, the bound alone decides.
A program may use at most 64 MiB of HBM per device.

v0:
```python
import functools

import jax
import jax.numpy as jnp
from jax import lax
from jax.experimental import pallas as pl
from jax.experimental.pallas import tpu as pltpu
from jax.sharding import PartitionSpec as P

OUTER = 2
INNER = 2
PIVOTS = 4
CHUNK = 128

HUBER = 1.345
RIDGE = 0.01

F32 = jnp.float32
BF16 = jnp.bfloat16
MESH = pl.DeviceIdType.MESH


def split(x):
    hi = x.astype(BF16)
    lo = (x - hi.astype(F32)).astype(BF16)
    return hi, lo


def dot(a, b):
    return jnp.dot(a, b, preferred_element_type=F32)


def quads(x):
    r, c = x.shape[0] // 2, x.shape[1] // 2
    return (x[:r, :c] + x[:r, c:]) + (x[r:, :c] + x[r:, c:])


def pts_peer(me, j, n):
    if n % 2:
        return lax.rem(me + j, n)
    x, c = me // 2, lax.rem(me, 2)
    return lax.rem(x + j // 2, n // 2) * 2 + lax.rem(c + lax.rem(j, 2), 2)


def snap_peer(me, j, n):
    return lax.rem(me + j, n)


def kernel(n_pts, n_snap, s_hbm, m_in, c_in, m_out, c_out,
           s, e, mcat, mtcat, ccat, ctcat, sq,
           gpart, gslots, gred, gfull, hpart, hslots, hred, hfull,
           tile_p, slots_p, tile_s, slots_s, cpart, cslots, xslots, ypart, yslots, zpart, zslots,
           load_sem, p_send, p_recv, s_send, s_recv, c_send, c_recv, x_send, x_recv,
           y_send, y_recv, z_send, z_recv):
    rows, width = s.shape
    rank = m_in.shape[1]
    pme = lax.axis_index("pts")
    sme = lax.axis_index("snap")
    rw = rows // n_snap
    half = width // 2
    chunks = half // CHUNK
    n_x, n_z = n_pts // 2, n_snap // 2
    px, core = pme // 2, lax.rem(pme, 2)
    sz, sy = sme // 2, lax.rem(sme, 2)
    gw = rank // n_pts
    hw = rank // n_snap
    count = float(rows * n_pts * width * n_snap)
    step_cols = 256

    load = pltpu.make_async_copy(s_hbm, s, load_sem)
    load.start()

    barrier = pltpu.get_barrier_semaphore()
    for j in range(1, n_pts):
        pl.semaphore_signal(barrier, inc=1, device_id={"pts": pts_peer(pme, j, n_pts)}, device_id_type=MESH)
    for j in range(1, n_snap):
        pl.semaphore_signal(barrier, inc=1, device_id={"snap": snap_peer(sme, j, n_snap)}, device_id_type=MESH)
    m_out[...] = m_in[...]
    c_out[...] = c_in[...]
    pl.semaphore_wait(barrier, n_pts - 1 + n_snap - 1)

    def pcopy(site, j, src, dst):
        return pltpu.make_async_remote_copy(
            src_ref=src, dst_ref=dst, send_sem=p_send.at[site, j - 1], recv_sem=p_recv.at[site, j - 1],
            device_id={"pts": pts_peer(pme, j, n_pts)}, device_id_type=MESH)

    def scopy(site, j, src, dst):
        return pltpu.make_async_remote_copy(
            src_ref=src, dst_ref=dst, send_sem=s_send.at[site, j - 1], recv_sem=s_recv.at[site, j - 1],
            device_id={"snap": snap_peer(sme, j, n_snap)}, device_id_type=MESH)

    def ccopy(site, k, src, dst):
        return pltpu.make_async_remote_copy(
            src_ref=src, dst_ref=dst, send_sem=c_send.at[site, k], recv_sem=c_recv.at[site, k],
            device_id={"pts": px * 2 + 1 - core}, device_id_type=MESH)

    def xcopy(site, k, d):
        ref = xslots.at[site, px, k]
        return pltpu.make_async_remote_copy(
            src_ref=ref, dst_ref=ref, send_sem=x_send.at[site, k, d - 1], recv_sem=x_recv.at[site, k, d - 1],
            device_id={"pts": lax.rem(px + d, n_x) * 2 + core}, device_id_type=MESH)

    def ycopy(site, d, src, dst):
        return pltpu.make_async_remote_copy(
            src_ref=src, dst_ref=dst, send_sem=y_send.at[site, d], recv_sem=y_recv.at[site, d],
            device_id={"snap": sz * 2 + 1 - sy}, device_id_type=MESH)

    def zcopy(site, d, src, dst):
        return pltpu.make_async_remote_copy(
            src_ref=src, dst_ref=dst, send_sem=z_send.at[site, d - 1], recv_sem=z_recv.at[site, d - 1],
            device_id={"snap": lax.rem(sz + d, n_z) * 2 + sy}, device_id_type=MESH)

    def col_chunk(which, k):
        return pl.ds(pl.multiple_of(which * half + k * CHUNK, CHUNK), CHUNK)

    def row_block(d, which):
        return pl.ds(pl.multiple_of((lax.rem(sz + d, n_z) * 2 + which) * rw, rw), rw)

    def start(copies):
        for copy in copies:
            copy.start()

    def finish(copies):
        for copy in copies:
            copy.wait_recv()
        for copy in copies:
            copy.wait_send()

    def prepare_modes():
        m = m_out[...]
        hi, lo = split(m)
        mcat[:, :rank] = hi
        mcat[:, rank:] = lo
        hi, lo = split(m.T)
        mtcat[:rank, :] = hi
        mtcat[rank:, :] = lo

    def prepare_coefs():
        hi, lo = split(c_out[...])
        ccat[:rank, :] = hi
        ccat[rank:, :] = lo

    def sweep(ref, base, steps):
        lane = lax.broadcasted_iota(jnp.int32, (rank, rank), 1)
        sub = lax.broadcasted_iota(jnp.int32, (rank, rank), 0)
        lane_row = lax.broadcasted_iota(jnp.int32, (1, rank), 1)
        sub_col = lax.broadcasted_iota(jnp.int32, (rank, 1), 0)

        def body(t, carry):
            k = (base + t) * PIVOTS
            full = ref[...]
            cols = [jnp.sum(jnp.where(lane == k + p, full, 0.0), axis=1, keepdims=True) for p in range(PIVOTS)]
            rws = [ref[pl.ds(k + p, 1), :] for p in range(PIVOTS)]
            blk = {}
            for p in range(PIVOTS):
                for q in range(p, PIVOTS):
                    blk[p, q] = jnp.sum(jnp.where(lane_row == k + q, rws[p], 0.0), axis=1, keepdims=True)
            for p in range(PIVOTS):
                inv = 1.0 / blk[p, p]
                row, col = rws[p], cols[p]
                for q in range(p + 1, PIVOTS):
                    f = blk[p, q] * inv
                    rws[q] = jnp.where(lane_row == k + p, f, rws[q] - f * row)
                    cols[q] = jnp.where(sub_col == k + p, f, cols[q] - f * col)
                    for u in range(q, PIVOTS):
                        blk[q, u] = blk[q, u] - f * blk[p, u]
                rowd = row * inv
                full = jnp.where(lane == k + p, col * inv, full - col * rowd)
                full = jnp.where(sub == k + p, jnp.where(lane_row == k + p, -inv, rowd), full)
            ref[...] = full
            return carry
        lax.fori_loop(0, steps, body, 0)

    def error_pass():
        sq[...] = jnp.zeros_like(sq)

        def body(t, carry):
            cols = pl.ds(pl.multiple_of(t * step_cols, step_cols), step_cols)
            c = ccat[:, cols]
            hi, lo = mcat[:, :rank], mcat[:, rank:]
            fit = dot(jnp.concatenate([hi, hi], 1), c) + dot(jnp.concatenate([lo, lo], 1), c)
            err = s[:, cols] - fit
            e[:, cols] = err
            sq[...] += jnp.sum((err * err).reshape(rows // 8, 8, step_cols), axis=0)
            return carry
        lax.fori_loop(0, width // step_cols, body, 0)
        acc = sq[:, :128]
        for k in range(1, step_cols // 128):
            acc = acc + sq[:, k * 128:(k + 1) * 128]
        return acc

    def find_limit(use, acc, fill_p, fill_s):
        tile_p[use] = acc
        copies = [pcopy(use, j, tile_p.at[use], slots_p.at[use, j - 1]) for j in range(1, n_pts)]
        start(copies)
        fill_p()
        finish(copies)
        acc = tile_p[use]
        for j in range(1, n_pts):
            acc = acc + slots_p[use, j - 1]
        tile_s[use] = acc
        copies = [scopy(use, j, tile_s.at[use], slots_s.at[use, j - 1]) for j in range(1, n_snap)]
        start(copies)
        fill_s()
        finish(copies)
        acc = tile_s[use]
        for j in range(1, n_snap):
            acc = acc + slots_s[use, j - 1]
        total = jnp.sum(jnp.sum(acc, axis=0, keepdims=True), axis=1, keepdims=True)
        return HUBER * jnp.sqrt(total / count + 1e-06)

    def nothing():
        return None

    eye = (lax.broadcasted_iota(jnp.int32, (rank, rank), 0)
           == lax.broadcasted_iota(jnp.int32, (rank, rank), 1)).astype(F32) * RIDGE

    prepare_modes()
    prepare_coefs()
    load.wait()

    def outer(o, carry):
        gpart[...] = quads(dot(mtcat[...], mcat[...]))
        grs = [pcopy(3, j, gpart.at[pl.ds(pts_peer(pme, j, n_pts) * gw, gw)], gslots.at[j - 1]) for j in range(1, n_pts)]
        start(grs)
        gag = [pcopy(4, j, gred, gfull.at[pl.ds(pme * gw, gw)]) for j in range(1, n_pts)]

        for inner in range(INNER):
            acc = error_pass()

            def gram_share():
                finish(grs)
                own = gpart[pl.ds(pme * gw, gw), :]
                for j in range(1, n_pts):
                    own = own + gslots[j - 1]
                gred[...] = own
                gfull[pl.ds(pme * gw, gw), :] = own
                start(gag)

            def gram_sweep():
                finish(gag)
                gfull[...] = gfull[...] + eye
                sweep(gfull, 0, rank // PIVOTS // 2)
            first = inner == 0
            limit = find_limit(inner, acc, gram_share if first else nothing, gram_sweep if first else nothing)

            def product(cols):
                hi, lo = split(jnp.clip(e[:, cols], -limit, limit))
                return quads(dot(mtcat[...], jnp.concatenate([hi, lo], 1)))

            def give(k):
                return ccopy(inner, k, cpart.at[k], cslots.at[inner, k])

            def spread(k):
                ref = c_out.at[:, col_chunk(core, k)]
                return ccopy(INNER + inner, k, ref, ref)

            def theirs(k, carry):
                cpart[k] = product(col_chunk(1 - core, k))
                give(k).start()
                return carry
            lax.fori_loop(0, chunks, theirs, 0)

            def ours(k, carry):
                mine = product(col_chunk(core, k))
                give(k).wait_recv()
                xslots[inner, px, k] = mine + cslots[inner, k]
                for d in range(1, n_x):
                    xcopy(inner, k, d).start()
                return carry
            lax.fori_loop(0, chunks, ours, 0)
            if first:
                sweep(gfull, rank // PIVOTS // 2, rank // PIVOTS // 2)

            def update(k, carry):
                for d in range(1, n_x):
                    xcopy(inner, k, d).wait_recv()
                share = xslots[inner, 0, k]
                for x in range(1, n_x):
                    share = share + xslots[inner, x, k]
                step = jnp.dot(gfull[...], share, preferred_element_type=F32, precision=lax.Precision.HIGHEST)
                cols = col_chunk(core, k)
                c_out[:, cols] = c_out[:, cols] - step
                spread(k).start()
                return carry
            lax.fori_loop(0, chunks, update, 0)

            def settle(k, carry):
                spread(k).wait_recv()
                spread(k).wait_send()
                give(k).wait_send()
                for d in range(1, n_x):
                    xcopy(inner, k, d).wait_send()
                return carry
            lax.fori_loop(0, chunks, settle, 0)
            prepare_coefs()

        hi, lo = split(c_out[...].T)
        ctcat[:, :rank] = hi
        ctcat[:, rank:] = lo
        hpart[...] = quads(dot(ccat[...], ctcat[...]))
        hrs = [scopy(3, j, hpart.at[pl.ds(snap_peer(sme, j, n_snap) * hw, hw)], hslots.at[j - 1]) for j in range(1, n_snap)]
        start(hrs)
        hag = [scopy(4, j, hred, hfull.at[pl.ds(sme * hw, hw)]) for j in range(1, n_snap)]

        def hess_share():
            finish(hrs)
            own = hpart[pl.ds(sme * hw, hw), :]
            for j in range(1, n_snap):
                own = own + hslots[j - 1]
            hred[...] = own
            hfull[pl.ds(sme * hw, hw), :] = own
            start(hag)
        limit = find_limit(2, error_pass(), hess_share, nothing)

        def moment(part):
            hi, lo = split(jnp.clip(e[part, :], -limit, limit))
            return quads(dot(jnp.concatenate([hi, lo], 0), ctcat[...]))

        def over_y(d):
            return ycopy(0, d, ypart.at[d], yslots.at[d])

        def over_z(d):
            return zcopy(0, d, zpart.at[d], zslots.at[d - 1])

        def theirs(t, carry):
            d = n_z - 1 - t
            ypart[d] = moment(row_block(d, 1 - sy))
            over_y(d).start()
            return carry
        lax.fori_loop(0, n_z, theirs, 0)

        finish(hag)
        hfull[...] = hfull[...] + eye
        early = rank // PIVOTS // 2 // n_z

        def ours(t, carry):
            d = n_z - 1 - t
            mine = moment(row_block(d, sy))
            sweep(hfull, t * early, early)
            over_y(d).wait_recv()
            zpart[d] = mine + yslots[d]

            @pl.when(d > 0)
            def _():
                over_z(d).start()
            return carry
        lax.fori_loop(0, n_z, ours, 0)
        sweep(hfull, early * n_z, rank // PIVOTS - early * n_z)
        for d in range(1, n_z):
            over_z(d).wait_recv()
        share = zpart[0]
        for d in range(1, n_z):
            share = share + zslots[d - 1]
        step = jnp.dot(share, hfull[...], preferred_element_type=F32, precision=lax.Precision.HIGHEST)
        own_rows = row_block(0, sy)
        m_out[own_rows, :] = m_out[own_rows, :] - step
        own_ref = m_out.at[own_rows]
        order = sorted(range(1, n_z), key=lambda d: -min(d, n_z - d))
        for d in order:
            zcopy(1, d, own_ref, own_ref).start()
        ycopy(1, 0, own_ref, own_ref).start()

        def pass_on(d):
            ref = m_out.at[row_block(n_z - d, sy)]
            return ycopy(1, d, ref, ref)
        for d in sorted(range(1, n_z), key=lambda d: min(d, n_z - d)):
            zcopy(1, d, own_ref, own_ref).wait_recv()
            pass_on(d).start()
        ycopy(1, 0, own_ref, own_ref).wait_recv()
        for d in range(1, n_z):
            pass_on(d).wait_recv()
        ycopy(1, 0, own_ref, own_ref).wait_send()
        over_y(0).wait_send()
        for d in range(1, n_z):
            pass_on(d).wait_send()
            over_y(d).wait_send()
            over_z(d).wait_send()
            zcopy(1, d, own_ref, own_ref).wait_send()

        @pl.when(o < OUTER - 1)
        def _():
            prepare_modes()
        return carry
    lax.fori_loop(0, OUTER, outer, 0)


def shards(n_pts, n_snap, snapshots, modes_init, coefs_init):
    rows, width = snapshots.shape
    rank = modes_init.shape[1]
    rw, gw, hw = rows // n_snap, rank // n_pts, rank // n_snap
    chunks, n_x, n_z = width // 2 // CHUNK, n_pts // 2, n_snap // 2
    points = float(rows * n_pts)
    vmem = pltpu.VMEM
    scratch = [
        vmem((rows, width), F32), vmem((rows, width), F32),
        vmem((rows, 2 * rank), BF16), vmem((2 * rank, rows), BF16),
        vmem((2 * rank, width), BF16), vmem((width, 2 * rank), BF16),
        vmem((8, 256), F32),
        vmem((rank, rank), F32), vmem((n_pts - 1, gw, rank), F32), vmem((gw, rank), F32), vmem((rank, rank), F32),
        vmem((rank, rank), F32), vmem((n_snap - 1, hw, rank), F32), vmem((hw, rank), F32), vmem((rank, rank), F32),
        vmem((3, 8, 128), F32), vmem((3, n_pts - 1, 8, 128), F32),
        vmem((3, 8, 128), F32), vmem((3, n_snap - 1, 8, 128), F32),
        vmem((chunks, rank, CHUNK), F32), vmem((INNER, chunks, rank, CHUNK), F32),
        vmem((INNER, n_x, chunks, rank, CHUNK), F32),
        vmem((n_z, rw, rank), F32), vmem((n_z, rw, rank), F32),
        vmem((n_z, rw, rank), F32), vmem((n_z - 1, rw, rank), F32),
        pltpu.SemaphoreType.DMA,
        pltpu.SemaphoreType.DMA((5, n_pts - 1)), pltpu.SemaphoreType.DMA((5, n_pts - 1)),
        pltpu.SemaphoreType.DMA((5, n_snap - 1)), pltpu.SemaphoreType.DMA((5, n_snap - 1)),
        pltpu.SemaphoreType.DMA((2 * INNER, chunks)), pltpu.SemaphoreType.DMA((2 * INNER, chunks)),
        pltpu.SemaphoreType.DMA((INNER, chunks, n_x - 1)), pltpu.SemaphoreType.DMA((INNER, chunks, n_x - 1)),
        pltpu.SemaphoreType.DMA((2, n_z)), pltpu.SemaphoreType.DMA((2, n_z)),
        pltpu.SemaphoreType.DMA((2, n_z - 1)), pltpu.SemaphoreType.DMA((2, n_z - 1)),
    ]
    modes, coefs = pl.pallas_call(
        functools.partial(kernel, n_pts, n_snap),
        out_shape=(jax.ShapeDtypeStruct((rows, rank), F32), jax.ShapeDtypeStruct((rank, width), F32)),
        in_specs=[pl.BlockSpec(memory_space=pl.ANY)] + [pl.BlockSpec(memory_space=vmem)] * 2,
        out_specs=(pl.BlockSpec(memory_space=vmem), pl.BlockSpec(memory_space=vmem)),
        scratch_shapes=scratch,
        compiler_params=pltpu.CompilerParams(collective_id=0, has_side_effects=True, vmem_limit_bytes=60 * 1024 * 1024),
    )(snapshots, modes_init, coefs_init)
    return modes, coefs * jnp.sqrt(jnp.float32(points))


def solution(mesh):
    in_specs = (P("pts", "snap"), P("pts", None), P(None, "snap"))
    out_specs = (P("pts", None), P(None, "snap"))
    body = functools.partial(shards, mesh.shape["pts"], mesh.shape["snap"])
    return jax.shard_map(body, mesh=mesh, in_specs=in_specs, out_specs=out_specs, check_vma=False)
```

profile of v0, /device:TPU:0, one launch (start us, length us, event | category | flops | bytes accessed | tf_op | source)
XLA Modules:
  0.0 152.5 jit_solution(10220369204819855213)
XLA Ops:
  0.6 148.2 %shard_map.50 = (f32[1024,128]{1,0:T(8,128)}, f32[128,1024]{1,0:T(8,128)}) custom-call(f32[1024,1024]{1,0:T(8,128)} %s_hbm.1, f32[1024,128]{1,0:T(8,128)} %m_in.1, f32[128,1024]{1,0:T(8,128)} %c_in.1), custom_call_target="tpu_custom_call" | custom-call | tf_op jit(solution)/shard_map/pallas_call | solution.py:416
  148.8 1.9 %broadcast_multiply_fusion = f32[128,1024]{1,0:T(8,128)} fusion(f32[128,1024]{1,0:T(8,128)} %get-tuple-element.5), kind=kLoop, calls=%fused_computation | loop fusion | flops 131072 | bytes 1048576 | tf_op jit(solution)/shard_map/mul | solution.py:424
  150.7 1.9 %copy.6 = f32[1024,128]{1,0:T(8,128)} copy(f32[1024,128]{1,0:T(8,128)} %get-tuple-element.8) | data formatting | bytes 1048576
where the time goes:
time: 153 us
  Pallas kernels  148 us (97%)
  other arithmetic  1.88 us (1%)
  local copies, waits for them, and re-layouts  1.87 us (1%)
    pallas_call x1, Pallas kernels, shards(): pl.pallas_call(functools.partial(kernel, n_pts, n_snap), out_shape=(jax.S...  148 us

commit v1 on v0

v1 whole, which is shorter than its diff:
```python
import functools

import jax
import jax.numpy as jnp
from jax import lax
from jax.experimental import pallas as pl
from jax.experimental.pallas import tpu as pltpu
from jax.sharding import PartitionSpec as P

OUTER = 2
INNER = 2
PIVOTS = 4
CHUNK = 128
STEP = 256

HUBER = 1.345
RIDGE = 0.01

F32 = jnp.float32
BF16 = jnp.bfloat16
MESH = pl.DeviceIdType.MESH


def split(x):
    hi = x.astype(BF16)
    lo = (x - hi.astype(F32)).astype(BF16)
    return hi, lo


def dot(a, b):
    return jnp.dot(a, b, preferred_element_type=F32)


def quads(x):
    r, c = x.shape[0] // 2, x.shape[1] // 2
    return (x[:r, :c] + x[:r, c:]) + (x[r:, :c] + x[r:, c:])


def pts_peer(me, j, n):
    if n % 2:
        return lax.rem(me + j, n)
    x, c = me // 2, lax.rem(me, 2)
    return lax.rem(x + j // 2, n // 2) * 2 + lax.rem(c + lax.rem(j, 2), 2)


def snap_peer(me, j, n):
    return lax.rem(me + j, n)


def kernel(n_pts, n_snap, s_hbm, m_hbm, c_hbm, m_out, c_out,
           s, e, mcat, mtcat, ccat, ctcat, sq,
           gpart, gslots, gred, gfull, hpart, hslots, hred, hfull,
           lslots, cpart, cslots, xslots, mpart, mslots,
           load_sem, p_send, p_recv, s_send, s_recv, c_send, c_recv, x_send, x_recv,
           l_send, l_recv, m_send, m_recv):
    rows, width = s.shape
    rank = m_out.shape[1]
    pme = lax.axis_index("pts")
    sme = lax.axis_index("snap")
    n_dev = n_pts * n_snap
    me = pme * n_snap + sme
    rw = rows // n_snap
    half = width // 2
    chunks = half // CHUNK
    n_x, n_z = n_pts // 2, n_snap // 2
    px, core = pme // 2, lax.rem(pme, 2)
    sz, sy = sme // 2, lax.rem(sme, 2)
    gw = rank // n_pts
    hw = rank // n_snap
    count = float(rows * n_pts * width * n_snap)
    loads = width // STEP

    def offset(d):
        dx, dc, dz, dy = d
        return {"pts": lax.rem(px + dx, n_x) * 2 + lax.rem(core + dc, 2),
                "snap": lax.rem(sz + dz, n_z) * 2 + lax.rem(sy + dy, 2)}

    def hops(d):
        dx, dc, dz, dy = d
        return min(dx, n_x - dx) + dy + min(dz, n_z - dz) + 0.1 * dc
    others = [(dx, dc, dz, dy) for dx in range(n_x) for dc in range(2) for dz in range(n_z) for dy in range(2)][1:]
    others.sort(key=lambda d: -hops(d))

    barrier = pltpu.get_barrier_semaphore()
    for d in others:
        pl.semaphore_signal(barrier, inc=1, device_id=offset(d), device_id_type=MESH)

    def load_cols(j):
        cols = pl.ds(j * STEP, STEP)
        return pltpu.make_async_copy(s_hbm.at[:, cols], s.at[:, cols], load_sem.at[2 + j])
    load_m = pltpu.make_async_copy(m_hbm, m_out, load_sem.at[0])
    load_c = pltpu.make_async_copy(c_hbm, c_out, load_sem.at[1])
    load_m.start()
    load_c.start()
    for j in range(loads):
        load_cols(j).start()

    def pcopy(site, j, src, dst):
        return pltpu.make_async_remote_copy(
            src_ref=src, dst_ref=dst, send_sem=p_send.at[site, j - 1], recv_sem=p_recv.at[site, j - 1],
            device_id={"pts": pts_peer(pme, j, n_pts)}, device_id_type=MESH)

    def scopy(site, j, src, dst):
        return pltpu.make_async_remote_copy(
            src_ref=src, dst_ref=dst, send_sem=s_send.at[site, j - 1], recv_sem=s_recv.at[site, j - 1],
            device_id={"snap": snap_peer(sme, j, n_snap)}, device_id_type=MESH)

    def ccopy(site, k, src, dst):
        return pltpu.make_async_remote_copy(
            src_ref=src, dst_ref=dst, send_sem=c_send.at[site, k], recv_sem=c_recv.at[site, k],
            device_id={"pts": px * 2 + 1 - core}, device_id_type=MESH)

    def xcopy(site, k, d):
        ref = xslots.at[site, px, k]
        return pltpu.make_async_remote_copy(
            src_ref=ref, dst_ref=ref, send_sem=x_send.at[site, k, d - 1], recv_sem=x_recv.at[site, k, d - 1],
            device_id={"pts": lax.rem(px + d, n_x) * 2 + core}, device_id_type=MESH)

    def lcopy(use, i):
        ref = lslots.at[use, pl.ds(me, 1)]
        return pltpu.make_async_remote_copy(
            src_ref=ref, dst_ref=ref, send_sem=l_send.at[use, i], recv_sem=l_recv.at[use, i],
            device_id=offset(others[i]), device_id_type=MESH)

    def shift(t):
        u = lax.rem(t, n_z)
        dz = n_z // 2 + ((u + 1) // 2) * (1 - 2 * lax.rem(u, 2))
        return dz, 1 - t // n_z

    def mcopy(site, t, src, dst):
        dz, dy = shift(t)
        return pltpu.make_async_remote_copy(
            src_ref=src, dst_ref=dst, send_sem=m_send.at[site, t], recv_sem=m_recv.at[site, t],
            device_id={"snap": lax.rem(sz + dz, n_z) * 2 + lax.rem(sy + dy, 2)}, device_id_type=MESH)

    def rows_to(t):
        dz, dy = shift(t)
        return pl.ds(pl.multiple_of((lax.rem(sz + dz, n_z) * 2 + lax.rem(sy + dy, 2)) * rw, rw), rw)

    def rows_from(t):
        dz, dy = shift(t)
        return pl.ds(pl.multiple_of((lax.rem(sz + n_z - dz, n_z) * 2 + lax.rem(sy + 2 - dy, 2)) * rw, rw), rw)

    def col_chunk(which, k):
        return pl.ds(pl.multiple_of(which * half + k * CHUNK, CHUNK), CHUNK)

    def start(copies):
        for copy in copies:
            copy.start()

    def finish(copies):
        for copy in copies:
            copy.wait_recv()
        for copy in copies:
            copy.wait_send()

    def prepare_rows(part):
        hi, lo = split(m_out[part, :])
        mcat[part, :rank] = hi
        mcat[part, rank:] = lo

    def prepare_mt():
        hi, lo = split(m_out[...].T)
        mtcat[:rank, :] = hi
        mtcat[rank:, :] = lo

    def prepare_cols(cols, value):
        hi, lo = split(value)
        ccat[:rank, cols] = hi
        ccat[rank:, cols] = lo

    def prepare_ct(cols, value):
        hi, lo = split(value.T)
        ctcat[cols, :rank] = hi
        ctcat[cols, rank:] = lo

    def sweep(ref, base, steps):
        lane = lax.broadcasted_iota(jnp.int32, (rank, rank), 1)
        sub = lax.broadcasted_iota(jnp.int32, (rank, rank), 0)
        lane_row = lax.broadcasted_iota(jnp.int32, (1, rank), 1)
        sub_col = lax.broadcasted_iota(jnp.int32, (rank, 1), 0)

        def body(t, carry):
            k = (base + t) * PIVOTS
            full = ref[...]
            cols = [jnp.sum(jnp.where(lane == k + p, full, 0.0), axis=1, keepdims=True) for p in range(PIVOTS)]
            rws = [ref[pl.ds(k + p, 1), :] for p in range(PIVOTS)]
            blk = {}
            for p in range(PIVOTS):
                for q in range(p, PIVOTS):
                    blk[p, q] = jnp.sum(jnp.where(lane_row == k + q, rws[p], 0.0), axis=1, keepdims=True)
            for p in range(PIVOTS):
                inv = 1.0 / blk[p, p]
                row, col = rws[p], cols[p]
                for q in range(p + 1, PIVOTS):
                    f = blk[p, q] * inv
                    rws[q] = jnp.where(lane_row == k + p, f, rws[q] - f * row)
                    cols[q] = jnp.where(sub_col == k + p, f, cols[q] - f * col)
                    for u in range(q, PIVOTS):
                        blk[q, u] = blk[q, u] - f * blk[p, u]
                rowd = row * inv
                full = jnp.where(lane == k + p, col * inv, full - col * rowd)
                full = jnp.where(sub == k + p, jnp.where(lane_row == k + p, -inv, rowd), full)
            ref[...] = full
            return carry
        with jax.named_scope("sweep"):
            lax.fori_loop(0, steps, body, 0)

    def errors(part, n_rows, cols):
        hi, lo = mcat[part, :rank], mcat[part, rank:]
        c = ccat[:, cols]
        fit = dot(jnp.concatenate([hi, hi], 1), c) + dot(jnp.concatenate([lo, lo], 1), c)
        err = s[part, cols] - fit
        e[part, cols] = err
        sq[...] += jnp.sum((err * err).reshape(n_rows // 8, 8, STEP), axis=0)

    def step_cols(j):
        return pl.ds(pl.multiple_of(j * STEP, STEP), STEP)

    def error_rows(part):
        def body(j, carry):
            errors(part, rw, step_cols(j))
            return carry
        lax.fori_loop(0, loads, body, 0)

    def send_limit(use):
        acc = sq[:, :128]
        for k in range(1, STEP // 128):
            acc = acc + sq[:, k * 128:(k + 1) * 128]
        lslots[use, pl.ds(me, 1), :] = jnp.sum(acc, axis=0, keepdims=True)
        start([lcopy(use, i) for i in range(n_dev - 1)])
        sq[...] = jnp.zeros_like(sq)

    def get_limit(use):
        with jax.named_scope("limit"):
            for i in reversed(range(n_dev - 1)):
                lcopy(use, i).wait_recv()
        total = jnp.sum(jnp.sum(lslots[use], axis=0, keepdims=True), axis=1, keepdims=True)
        for i in range(n_dev - 1):
            lcopy(use, i).wait_send()
        return HUBER * jnp.sqrt(total / count + 1e-06)

    eye = (lax.broadcasted_iota(jnp.int32, (rank, rank), 0)
           == lax.broadcasted_iota(jnp.int32, (rank, rank), 1)).astype(F32) * RIDGE

    grs = [pcopy(0, j, gpart.at[pl.ds(pts_peer(pme, j, n_pts) * gw, gw)], gslots.at[j - 1]) for j in range(1, n_pts)]
    gag = [pcopy(1, j, gred, gfull.at[pl.ds(pme * gw, gw)]) for j in range(1, n_pts)]
    hrs = [scopy(0, j, hpart.at[pl.ds(snap_peer(sme, j, n_snap) * hw, hw)], hslots.at[j - 1]) for j in range(1, n_snap)]
    hag = [scopy(1, j, hred, hfull.at[pl.ds(sme * hw, hw)]) for j in range(1, n_snap)]
    own_rows = pl.ds(pl.multiple_of(sme * rw, rw), rw)

    def gram_part():
        prepare_mt()
        gpart[...] = quads(dot(mtcat[...], mcat[...]))

    sq[...] = jnp.zeros_like(sq)
    load_m.wait()
    prepare_rows(pl.ds(0, rows))
    gram_part()
    load_c.wait()
    prepare_cols(pl.ds(0, width), c_out[...])
    with jax.named_scope("barrier"):
        pl.semaphore_wait(barrier, n_dev - 1)
    start(grs)
    for j in range(loads):
        load_cols(j).wait()
    with jax.named_scope("err0"):
        def first(j, carry):
            errors(pl.ds(0, rows), rows, step_cols(j))
            return carry
        lax.fori_loop(0, loads, first, 0)
    send_limit(0)

    def outer(o, carry):
        more = o < OUTER - 1
        finish(grs)
        own = gpart[pl.ds(pme * gw, gw), :]
        for j in range(1, n_pts):
            own = own + gslots[j - 1]
        gred[...] = own
        gfull[pl.ds(pme * gw, gw), :] = own
        start(gag)

        for inner in range(INNER):
            limit = get_limit(inner)

            def give(k):
                return ccopy(inner, k, cpart.at[k], cslots.at[inner, k])

            def spread(k):
                ref = c_out.at[:, col_chunk(core, k)]
                return ccopy(INNER + inner, k, ref, ref)

            def products(t, carry):
                last = t == 2 * chunks - 1
                theirs = (t == 0) | ((lax.rem(t, 2) == 1) & (t < 2 * chunks - 1))
                k = jnp.where(theirs, (t + 1) // 2, jnp.where(last, chunks - 1, t // 2 - 1))
                which = jnp.where(theirs, 1 - core, core)
                hi, lo = split(jnp.clip(e[:, col_chunk(which, k)], -limit, limit))
                value = quads(dot(mtcat[...], jnp.concatenate([hi, lo], 1)))

                @pl.when(theirs)
                def _():
                    cpart[k] = value
                    give(k).start()

                @pl.when(jnp.logical_not(theirs))
                def _():
                    give(k).wait_recv()
                    xslots[inner, px, k] = value + cslots[inner, k]
                    for d in range(1, n_x):
                        xcopy(inner, k, d).start()
                return carry
            with jax.named_scope("products"):
                lax.fori_loop(0, 2 * chunks, products, 0)
            if inner == 0:
                finish(gag)
                gfull[...] = gfull[...] + eye
                sweep(gfull, 0, rank // PIVOTS)

            def update(t, carry):
                j = t // 2
                mine = lax.rem(t, 2) == 0
                per = STEP // CHUNK

                def own_cols(i, carry):
                    k = j * per + i
                    for d in range(1, n_x):
                        xcopy(inner, k, d).wait_recv()
                    share = xslots[inner, 0, k]
                    for x in range(1, n_x):
                        share = share + xslots[inner, x, k]
                    step = jnp.dot(gfull[...], share, preferred_element_type=F32, precision=lax.Precision.HIGHEST)
                    cols = col_chunk(core, k)
                    value = c_out[:, cols] - step
                    c_out[:, cols] = value
                    spread(k).start()
                    prepare_cols(cols, value)
                    if inner == INNER - 1:
                        prepare_ct(cols, value)
                    return carry

                def their_cols(i, carry):
                    k = j * per + i
                    spread(k).wait_recv()
                    cols = col_chunk(1 - core, k)
                    value = c_out[:, cols]
                    prepare_cols(cols, value)
                    if inner == INNER - 1:
                        prepare_ct(cols, value)
                    return carry

                @pl.when(mine)
                def _():
                    lax.fori_loop(0, per, own_cols, 0)

                @pl.when(jnp.logical_not(mine))
                def _():
                    lax.fori_loop(0, per, their_cols, 0)
                which = jnp.where(mine, core, 1 - core)
                with jax.named_scope("errchunk"):
                    errors(pl.ds(0, rows), rows, pl.ds(pl.multiple_of(which * half + j * STEP, STEP), STEP))
                return carry
            with jax.named_scope("update"):
                lax.fori_loop(0, loads, update, 0)
            send_limit(inner + 1)

            def settle(k, carry):
                spread(k).wait_send()
                give(k).wait_send()
                for d in range(1, n_x):
                    xcopy(inner, k, d).wait_send()
                return carry
            lax.fori_loop(0, chunks, settle, 0)

        with jax.named_scope("hpart"):
            hpart[...] = quads(dot(ccat[...], ctcat[...]))
            start(hrs)
        with jax.named_scope("hrs"):
            finish(hrs)
        own = hpart[pl.ds(sme * hw, hw), :]
        for j in range(1, n_snap):
            own = own + hslots[j - 1]
        hred[...] = own
        hfull[pl.ds(sme * hw, hw), :] = own
        start(hag)
        limit = get_limit(INNER)

        def moment(part):
            hi, lo = split(jnp.clip(e[part, :], -limit, limit))
            return quads(dot(jnp.concatenate([hi, lo], 0), ctcat[...]))

        def reduce_to(t):
            return mcopy(0, t, mpart.at[t], mslots.at[t])

        def gather(t):
            ref = m_out.at[own_rows]
            return mcopy(1, t, ref, ref)

        def moments(t, carry):
            mpart[t] = moment(rows_to(t))

            @pl.when(t < n_snap - 1)
            def _():
                reduce_to(t).start()
            return carry
        with jax.named_scope("moments"):
            lax.fori_loop(0, n_snap, moments, 0)
        with jax.named_scope("hag"):
            finish(hag)
        hfull[...] = hfull[...] + eye
        sweep(hfull, 0, rank // PIVOTS)
        with jax.named_scope("mwait"):
            for t in range(n_snap - 1):
                reduce_to(t).wait_recv()
        share = mpart[n_snap - 1]
        for t in range(n_snap - 1):
            share = share + mslots[t]
        step = jnp.dot(share, hfull[...], preferred_element_type=F32, precision=lax.Precision.HIGHEST)
        m_out[own_rows, :] = m_out[own_rows, :] - step
        start([gather(t) for t in range(n_snap - 1)])

        @pl.when(more)
        def _():
            prepare_rows(own_rows)
            error_rows(own_rows)

        def arrivals(u, carry):
            t = n_snap - 2 - u
            gather(t).wait_recv()

            @pl.when(more)
            def _():
                prepare_rows(rows_from(t))
                error_rows(rows_from(t))
            return carry
        with jax.named_scope("arrivals"):
            lax.fori_loop(0, n_snap - 1, arrivals, 0)

        @pl.when(more)
        def _():
            send_limit(0)
            gram_part()
            start(grs)
        for t in range(n_snap - 1):
            reduce_to(t).wait_send()
            gather(t).wait_send()
        return carry
    lax.fori_loop(0, OUTER, outer, 0)


def shards(n_pts, n_snap, snapshots, modes_init, coefs_init):
    rows, width = snapshots.shape
    rank = modes_init.shape[1]
    rw, gw, hw = rows // n_snap, rank // n_pts, rank // n_snap
    chunks, n_x, n_dev = width // 2 // CHUNK, n_pts // 2, n_pts * n_snap
    points = float(rows * n_pts)
    vmem, dma = pltpu.VMEM, pltpu.SemaphoreType.DMA
    scratch = [
        vmem((rows, width), F32), vmem((rows, width), F32),
        vmem((rows, 2 * rank), BF16), vmem((2 * rank, rows), BF16),
        vmem((2 * rank, width), BF16), vmem((width, 2 * rank), BF16),
        vmem((8, STEP), F32),
        vmem((rank, rank), F32), vmem((n_pts - 1, gw, rank), F32), vmem((gw, rank), F32), vmem((rank, rank), F32),
        vmem((rank, rank), F32), vmem((n_snap - 1, hw, rank), F32), vmem((hw, rank), F32), vmem((rank, rank), F32),
        vmem((INNER + 1, n_dev, 128), F32),
        vmem((chunks, rank, CHUNK), F32), vmem((INNER, chunks, rank, CHUNK), F32),
        vmem((INNER, n_x, chunks, rank, CHUNK), F32),
        vmem((n_snap, rw, rank), F32), vmem((n_snap - 1, rw, rank), F32),
        dma((2 + width // STEP,)),
        dma((2, n_pts - 1)), dma((2, n_pts - 1)),
        dma((2, n_snap - 1)), dma((2, n_snap - 1)),
        dma((2 * INNER, chunks)), dma((2 * INNER, chunks)),
        dma((INNER, chunks, n_x - 1)), dma((INNER, chunks, n_x - 1)),
        dma((INNER + 1, n_dev - 1)), dma((INNER + 1, n_dev - 1)),
        dma((2, n_snap - 1)), dma((2, n_snap - 1)),
    ]
    modes, coefs = pl.pallas_call(
        functools.partial(kernel, n_pts, n_snap),
        out_shape=(jax.ShapeDtypeStruct((rows, rank), F32), jax.ShapeDtypeStruct((rank, width), F32)),
        in_specs=[pl.BlockSpec(memory_space=pl.ANY)] * 3,
        out_specs=(pl.BlockSpec(memory_space=vmem), pl.BlockSpec(memory_space=vmem)),
        scratch_shapes=scratch,
        compiler_params=pltpu.CompilerParams(collective_id=0, has_side_effects=True, vmem_limit_bytes=60 * 1024 * 1024),
    )(snapshots, modes_init, coefs_init)
    return modes, coefs * jnp.sqrt(jnp.float32(points))


def solution(mesh):
    in_specs = (P("pts", "snap"), P("pts", None), P(None, "snap"))
    out_specs = (P("pts", None), P(None, "snap"))
    body = functools.partial(shards, mesh.shape["pts"], mesh.shape["snap"])
    return jax.shard_map(body, mesh=mesh, in_specs=in_specs, out_specs=out_specs, check_vma=False)
```

time: 153 us -> 151 us (0.987)
  Pallas kernels: 148 us -> 146 us
    pallas_call x1, Pallas kernels: 148 us -> 146 us  [shards(): pl.pallas_call(functools.partial(kernel, n_pts, n_snap), out_shape=(jax.S...]
where the time goes in v1:
time: 151 us
  Pallas kernels  146 us (97%)
  other arithmetic  1.88 us (1%)
  local copies, waits for them, and re-layouts  1.87 us (1%)
    pallas_call x1, Pallas kernels, shards(): pl.pallas_call(functools.partial(kernel, n_pts, n_snap), out_shape=(jax.S...  146 us

profile of v1, /device:TPU:0, one launch (start us, length us, event | category | flops | bytes accessed | tf_op | source)
XLA Modules:
  0.0 150.6 jit_solution(16196288360860497872)
XLA Ops:
  0.6 146.2 %shard_map.50 = (f32[1024,128]{1,0:T(8,128)}, f32[128,1024]{1,0:T(8,128)}) custom-call(f32[1024,1024]{1,0:T(8,128)} %s_hbm.1, f32[1024,128]{1,0:T(8,128)} %m_hbm.1, f32[128,1024]{1,0:T(8,128)} %c_hbm.1), custom_call_target="tpu_custom_call" | custom-call | tf_op jit(solution)/shard_map/pallas_call | solution.py:478
  146.9 1.9 %broadcast_multiply_fusion = f32[128,1024]{1,0:T(8,128)} fusion(f32[128,1024]{1,0:T(8,128)} %get-tuple-element.5), kind=kLoop, calls=%fused_computation | loop fusion | flops 131072 | bytes 1048576 | tf_op jit(solution)/shard_map/mul | solution.py:486
  148.8 1.9 %copy.6 = f32[1024,128]{1,0:T(8,128)} copy(f32[1024,128]{1,0:T(8,128)} %get-tuple-element.8) | data formatting | bytes 1048576

commit v2 on v1

--- a/solution.py
+++ b/solution.py
@@ -9,7 +9,7 @@
 
 OUTER = 2
 INNER = 2
-PIVOTS = 4
+PIVOTS = 16
 CHUNK = 128
 STEP = 256
 
@@ -25,6 +25,14 @@
     hi = x.astype(BF16)
     lo = (x - hi.astype(F32)).astype(BF16)
     return hi, lo
+
+
+def split3(x):
+    hi = x.astype(BF16)
+    rest = x - hi.astype(F32)
+    mid = rest.astype(BF16)
+    lo = (rest - mid.astype(F32)).astype(BF16)
+    return hi, mid, lo
 
 
 def dot(a, b):
@@ -50,9 +58,9 @@
 def kernel(n_pts, n_snap, s_hbm, m_hbm, c_hbm, m_out, c_out,
            s, e, mcat, mtcat, ccat, ctcat, sq,
            gpart, gslots, gred, gfull, hpart, hslots, hred, hfull,
-           lslots, cpart, cslots, xslots, mpart, mslots,
+           lslots, cpart, cslots, xslots, ypart, yslots, zpart, zslots,
            load_sem, p_send, p_recv, s_send, s_recv, c_send, c_recv, x_send, x_recv,
-           l_send, l_recv, m_send, m_recv):
+           l_send, l_recv, y_send, y_recv, z_send, z_recv):
     rows, width = s.shape
     rank = m_out.shape[1]
     pme = lax.axis_index("pts")
@@ -122,24 +130,21 @@
             src_ref=ref, dst_ref=ref, send_sem=l_send.at[use, i], recv_sem=l_recv.at[use, i],
             device_id=offset(others[i]), device_id_type=MESH)
 
-    def shift(t):
-        u = lax.rem(t, n_z)
-        dz = n_z // 2 + ((u + 1) // 2) * (1 - 2 * lax.rem(u, 2))
-        return dz, 1 - t // n_z
-
-    def mcopy(site, t, src, dst):
-        dz, dy = shift(t)
-        return pltpu.make_async_remote_copy(
-            src_ref=src, dst_ref=dst, send_sem=m_send.at[site, t], recv_sem=m_recv.at[site, t],
-            device_id={"snap": lax.rem(sz + dz, n_z) * 2 + lax.rem(sy + dy, 2)}, device_id_type=MESH)
-
-    def rows_to(t):
-        dz, dy = shift(t)
-        return pl.ds(pl.multiple_of((lax.rem(sz + dz, n_z) * 2 + lax.rem(sy + dy, 2)) * rw, rw), rw)
-
-    def rows_from(t):
-        dz, dy = shift(t)
-        return pl.ds(pl.multiple_of((lax.rem(sz + n_z - dz, n_z) * 2 + lax.rem(sy + 2 - dy, 2)) * rw, rw), rw)
+    def ycopy(site, d, src, dst):
+        return pltpu.make_async_remote_copy(
+            src_ref=src, dst_ref=dst, send_sem=y_send.at[site, d], recv_sem=y_recv.at[site, d],
+            device_id={"snap": sz * 2 + 1 - sy}, device_id_type=MESH)
+
+    def zcopy(site, d, src, dst):
+        return pltpu.make_async_remote_copy(
+            src_ref=src, dst_ref=dst, send_sem=z_send.at[site, d - 1], recv_sem=z_recv.at[site, d - 1],
+            device_id={"snap": lax.rem(sz + d, n_z) * 2 + sy}, device_id_type=MESH)
+
+    def row_block(d, which):
+        return pl.ds(pl.multiple_of((lax.rem(sz + d, n_z) * 2 + which) * rw, rw), rw)
+
+    def far(t):
+        return n_z // 2 + ((t + 1) // 2) * (1 - 2 * (t % 2))
 
     def col_chunk(which, k):
         return pl.ds(pl.multiple_of(which * half + k * CHUNK, CHUNK), CHUNK)
@@ -175,33 +180,33 @@
         ctcat[cols, rank:] = lo
 
     def sweep(ref, base, steps):
-        lane = lax.broadcasted_iota(jnp.int32, (rank, rank), 1)
-        sub = lax.broadcasted_iota(jnp.int32, (rank, rank), 0)
-        lane_row = lax.broadcasted_iota(jnp.int32, (1, rank), 1)
-        sub_col = lax.broadcasted_iota(jnp.int32, (rank, 1), 0)
+        sub = lax.broadcasted_iota(jnp.int32, (PIVOTS, rank), 0)
+        lane = lax.broadcasted_iota(jnp.int32, (PIVOTS, rank), 1)
+        wide = lax.broadcasted_iota(jnp.int32, (rank, rank), 1)
+        side = sub[:, :1]
 
         def body(t, carry):
             k = (base + t) * PIVOTS
-            full = ref[...]
-            cols = [jnp.sum(jnp.where(lane == k + p, full, 0.0), axis=1, keepdims=True) for p in range(PIVOTS)]
-            rws = [ref[pl.ds(k + p, 1), :] for p in range(PIVOTS)]
-            blk = {}
+            rws = pl.ds(pl.multiple_of(k, PIVOTS), PIVOTS)
+            before = ref[rws, :]
+            after = before
+            cols = [jnp.sum(jnp.where(lane == k + p, before, 0.0), axis=1, keepdims=True) for p in range(PIVOTS)]
             for p in range(PIVOTS):
-                for q in range(p, PIVOTS):
-                    blk[p, q] = jnp.sum(jnp.where(lane_row == k + q, rws[p], 0.0), axis=1, keepdims=True)
-            for p in range(PIVOTS):
-                inv = 1.0 / blk[p, p]
-                row, col = rws[p], cols[p]
+                col = cols[p]
+                inv = 1.0 / col[p:p + 1, :]
+                row = after[p:p + 1, :] * inv
                 for q in range(p + 1, PIVOTS):
-                    f = blk[p, q] * inv
-                    rws[q] = jnp.where(lane_row == k + p, f, rws[q] - f * row)
-                    cols[q] = jnp.where(sub_col == k + p, f, cols[q] - f * col)
-                    for u in range(q, PIVOTS):
-                        blk[q, u] = blk[q, u] - f * blk[p, u]
-                rowd = row * inv
-                full = jnp.where(lane == k + p, col * inv, full - col * rowd)
-                full = jnp.where(sub == k + p, jnp.where(lane_row == k + p, -inv, rowd), full)
-            ref[...] = full
+                    f = cols[q][p:p + 1, :] * inv
+                    cols[q] = jnp.where(side == p, f, cols[q] - col * f)
+                after = jnp.where(lane == k + p, col * inv, after - col * row)
+                after = jnp.where(sub == p, jnp.where(lane == k + p, -inv, row), after)
+            h, m, l = split3(before)
+            a, b, c = split3(after)
+            change = lax.dot_general(
+                jnp.concatenate([h, h, m, h, m, l], 0), jnp.concatenate([a, b, a, c, b, a], 0),
+                (((0,), (0,)), ((), ())), preferred_element_type=F32)
+            ref[...] = jnp.where((wide >= k) & (wide < k + PIVOTS), 0.0, ref[...]) - change
+            ref[rws, :] = after
             return carry
         with jax.named_scope("sweep"):
             lax.fori_loop(0, steps, body, 0)
@@ -218,10 +223,14 @@
         return pl.ds(pl.multiple_of(j * STEP, STEP), STEP)
 
     def error_rows(part):
-        def body(j, carry):
-            errors(part, rw, step_cols(j))
-            return carry
-        lax.fori_loop(0, loads, body, 0)
+        hi, lo = mcat[part, :rank], mcat[part, rank:]
+        both = jnp.concatenate([jnp.concatenate([hi, hi], 1), jnp.concatenate([lo, lo], 1)], 0)
+        for j in range(loads):
+            cols = pl.ds(j * STEP, STEP)
+            fit = dot(both, ccat[:, cols])
+            err = s[part, cols] - (fit[:rw] + fit[rw:])
+            e[part, cols] = err
+            sq[...] += jnp.sum((err * err).reshape(rw // 8, 8, STEP), axis=0)
 
     def send_limit(use):
         acc = sq[:, :128]
@@ -282,6 +291,12 @@
         start(gag)
 
         for inner in range(INNER):
+            if inner == 0:
+                @pl.when(o == 0)
+                def _():
+                    finish(gag)
+                    gfull[...] = gfull[...] + eye
+                    sweep(gfull, 0, rank // PIVOTS // 2)
             limit = get_limit(inner)
 
             def give(k):
@@ -314,9 +329,12 @@
             with jax.named_scope("products"):
                 lax.fori_loop(0, 2 * chunks, products, 0)
             if inner == 0:
-                finish(gag)
-                gfull[...] = gfull[...] + eye
-                sweep(gfull, 0, rank // PIVOTS)
+                @pl.when(o > 0)
+                def _():
+                    finish(gag)
+                    gfull[...] = gfull[...] + eye
+                    sweep(gfull, 0, rank // PIVOTS // 2)
+                sweep(gfull, rank // PIVOTS // 2, rank // PIVOTS // 2)
 
             def update(t, carry):
                 j = t // 2
@@ -376,75 +394,120 @@
         with jax.named_scope("hpart"):
             hpart[...] = quads(dot(ccat[...], ctcat[...]))
             start(hrs)
-        with jax.named_scope("hrs"):
-            finish(hrs)
-        own = hpart[pl.ds(sme * hw, hw), :]
-        for j in range(1, n_snap):
-            own = own + hslots[j - 1]
-        hred[...] = own
-        hfull[pl.ds(sme * hw, hw), :] = own
-        start(hag)
         limit = get_limit(INNER)
 
         def moment(part):
             hi, lo = split(jnp.clip(e[part, :], -limit, limit))
             return quads(dot(jnp.concatenate([hi, lo], 0), ctcat[...]))
 
-        def reduce_to(t):
-            return mcopy(0, t, mpart.at[t], mslots.at[t])
-
-        def gather(t):
-            ref = m_out.at[own_rows]
-            return mcopy(1, t, ref, ref)
+        def over_y(d):
+            return ycopy(0, d, ypart.at[d], yslots.at[d])
+
+        def over_z(d):
+            return zcopy(0, d, zpart.at[d], zslots.at[d - 1])
 
         def moments(t, carry):
-            mpart[t] = moment(rows_to(t))
-
-            @pl.when(t < n_snap - 1)
+            theirs = t < n_z
+            d = far(t % n_z)
+            value = moment(row_block(d, jnp.where(theirs, 1 - sy, sy)))
+
+            @pl.when(theirs)
             def _():
-                reduce_to(t).start()
+                ypart[d] = value
+                over_y(d).start()
+
+            @pl.when(jnp.logical_not(theirs))
+            def _():
+                zpart[d] = value
+
+            @pl.when(t == 0)
+            def _():
+                finish(hrs)
+                own = hpart[pl.ds(sme * hw, hw), :]
+                for j in range(1, n_snap):
+                    own = own + hslots[j - 1]
+                hred[...] = own
+                hfull[pl.ds(sme * hw, hw), :] = own
+                start(hag)
             return carry
         with jax.named_scope("moments"):
-            lax.fori_loop(0, n_snap, moments, 0)
-        with jax.named_scope("hag"):
-            finish(hag)
-        hfull[...] = hfull[...] + eye
-        sweep(hfull, 0, rank // PIVOTS)
-        with jax.named_scope("mwait"):
-            for t in range(n_snap - 1):
-                reduce_to(t).wait_recv()
-        share = mpart[n_snap - 1]
-        for t in range(n_snap - 1):
-            share = share + mslots[t]
+            lax.fori_loop(0, 2 * n_z, moments, 0)
+        steps = rank // PIVOTS
+
+        def forward(t, carry):
+            d = far(t)
+            with jax.named_scope("ywait"):
+                over_y(d).wait_recv()
+            zpart[d] = zpart[d] + yslots[d]
+
+            @pl.when(t < n_z - 1)
+            def _():
+                over_z(d).start()
+
+            @pl.when(t == 0)
+            def _():
+                with jax.named_scope("hag"):
+                    finish(hag)
+                hfull[...] = hfull[...] + eye
+            sweep(hfull, t * (steps // n_z), steps // n_z)
+            return carry
+        lax.fori_loop(0, n_z, forward, 0)
+        sweep(hfull, steps // n_z * n_z, steps - steps // n_z * n_z)
+        with jax.named_scope("zwait"):
+            for d in range(1, n_z):
+                over_z(d).wait_recv()
+        share = zpart[0]
+        for d in range(1, n_z):
+            share = share + zslots[d - 1]
         step = jnp.dot(share, hfull[...], preferred_element_type=F32, precision=lax.Precision.HIGHEST)
         m_out[own_rows, :] = m_out[own_rows, :] - step
-        start([gather(t) for t in range(n_snap - 1)])
-
-        @pl.when(more)
-        def _():
-            prepare_rows(own_rows)
-            error_rows(own_rows)
-
-        def arrivals(u, carry):
-            t = n_snap - 2 - u
-            gather(t).wait_recv()
-
+        own_ref = m_out.at[own_rows]
+        order = [far(t) for t in range(n_z - 1)]
+        start([zcopy(1, d, own_ref, own_ref) for d in order])
+        ycopy(1, 0, own_ref, own_ref).start()
+
+        def pass_on(d):
+            ref = m_out.at[row_block(n_z - d, sy)]
+            return ycopy(1, d, ref, ref)
+
+        def take(part):
             @pl.when(more)
             def _():
-                prepare_rows(rows_from(t))
-                error_rows(rows_from(t))
+                prepare_rows(part)
+                error_rows(part)
+        take(own_rows)
+        with jax.named_scope("gatherz"):
+            for d in order[::-1]:
+                zcopy(1, d, own_ref, own_ref).wait_recv()
+                pass_on(d).start()
+
+        def near(u, carry):
+            take(row_block(u, sy))
             return carry
-        with jax.named_scope("arrivals"):
-            lax.fori_loop(0, n_snap - 1, arrivals, 0)
+        with jax.named_scope("near"):
+            lax.fori_loop(1, n_z, near, 0)
+
+        def other(u, carry):
+            d = jnp.where(u == 0, 0, far(n_z - 1 - u))
+            with jax.named_scope("gathery"):
+                pass_on(d).wait_recv()
+            take(row_block(n_z - d, 1 - sy))
+            return carry
+        with jax.named_scope("other"):
+            lax.fori_loop(0, n_z, other, 0)
 
         @pl.when(more)
         def _():
             send_limit(0)
             gram_part()
             start(grs)
-        for t in range(n_snap - 1):
-            reduce_to(t).wait_send()
-            gather(t).wait_send()
+        ycopy(1, 0, own_ref, own_ref).wait_send()
+        over_y(0).wait_send()
+        for d in range(1, n_z):
+            pass_on(d).wait_send()
+            over_y(d).wait_send()
+            over_z(d).wait_send()
+            zcopy(1, d, own_ref, own_ref).wait_send()
         return carry
     lax.fori_loop(0, OUTER, outer, 0)
 
@@ -453,7 +516,7 @@
     rows, width = snapshots.shape
     rank = modes_init.shape[1]
     rw, gw, hw = rows // n_snap, rank // n_pts, rank // n_snap
-    chunks, n_x, n_dev = width // 2 // CHUNK, n_pts // 2, n_pts * n_snap
+    chunks, n_x, n_z, n_dev = width // 2 // CHUNK, n_pts // 2, n_snap // 2, n_pts * n_snap
     points = float(rows * n_pts)
     vmem, dma = pltpu.VMEM, pltpu.SemaphoreType.DMA
     scratch = [
@@ -466,14 +529,16 @@
         vmem((INNER + 1, n_dev, 128), F32),
         vmem((chunks, rank, CHUNK), F32), vmem((INNER, chunks, rank, CHUNK), F32),
         vmem((INNER, n_x, chunks, rank, CHUNK), F32),
-        vmem((n_snap, rw, rank), F32), vmem((n_snap - 1, rw, rank), F32),
+        vmem((n_z, rw, rank), F32), vmem((n_z, rw, rank), F32),
+        vmem((n_z, rw, rank), F32), vmem((n_z - 1, rw, rank), F32),
         dma((2 + width // STEP,)),
         dma((2, n_pts - 1)), dma((2, n_pts - 1)),
         dma((2, n_snap - 1)), dma((2, n_snap - 1)),
         dma((2 * INNER, chunks)), dma((2 * INNER, chunks)),
         dma((INNER, chunks, n_x - 1)), dma((INNER, chunks, n_x - 1)),
         dma((INNER + 1, n_dev - 1)), dma((INNER + 1, n_dev - 1)),
-        dma((2, n_snap - 1)), dma((2, n_snap - 1)),
+        dma((2, n_z)), dma((2, n_z)),
+        dma((2, n_z - 1)), dma((2, n_z - 1)),
     ]
     modes, coefs = pl.pallas_call(
         functools.partial(kernel, n_pts, n_snap),

time: 151 us -> 131 us (0.87)
  Pallas kernels: 146 us -> 126 us
    pallas_call x1, Pallas kernels: 146 us -> 126 us  [shards(): pl.pallas_call(functools.partial(kernel, n_pts, n_snap), out_shape=(jax.S...]
where the time goes in v2:
time: 131 us
  Pallas kernels  126 us (96%)
  other arithmetic  1.88 us (1%)
  local copies, waits for them, and re-layouts  1.87 us (1%)
    pallas_call x1, Pallas kernels, shards(): pl.pallas_call(functools.partial(kernel, n_pts, n_snap), out_shape=(jax.S...  126 us

profile of v2, /device:TPU:0, one launch (start us, length us, event | category | flops | bytes accessed | tf_op | source)
XLA Modules:
  0.0 130.6 jit_solution(15512664526777408961)
XLA Ops:
  0.6 126.2 %shard_map.50 = (f32[1024,128]{1,0:T(8,128)}, f32[128,1024]{1,0:T(8,128)}) custom-call(f32[1024,1024]{1,0:T(8,128)} %s_hbm.1, f32[1024,128]{1,0:T(8,128)} %m_hbm.1, f32[128,1024]{1,0:T(8,128)} %c_hbm.1), custom_call_target="tpu_custom_call" | custom-call | tf_op jit(solution)/shard_map/pallas_call | solution.py:543
  126.8 1.9 %broadcast_multiply_fusion = f32[128,1024]{1,0:T(8,128)} fusion(f32[128,1024]{1,0:T(8,128)} %get-tuple-element.5), kind=kLoop, calls=%fused_computation | loop fusion | flops 131072 | bytes 1048576 | tf_op jit(solution)/shard_map/mul | solution.py:551
  128.7 1.9 %copy.6 = f32[1024,128]{1,0:T(8,128)} copy(f32[1024,128]{1,0:T(8,128)} %get-tuple-element.8) | data formatting | bytes 1048576

commit v3 on v2

--- a/solution.py
+++ b/solution.py
@@ -93,8 +93,11 @@
     for d in others:
         pl.semaphore_signal(barrier, inc=1, device_id=offset(d), device_id_type=MESH)
 
+    def step_cols(j):
+        return pl.ds(pl.multiple_of(j * STEP, STEP), STEP)
+
     def load_cols(j):
-        cols = pl.ds(j * STEP, STEP)
+        cols = step_cols(j)
         return pltpu.make_async_copy(s_hbm.at[:, cols], s.at[:, cols], load_sem.at[2 + j])
     load_m = pltpu.make_async_copy(m_hbm, m_out, load_sem.at[0])
     load_c = pltpu.make_async_copy(c_hbm, c_out, load_sem.at[1])
@@ -121,14 +124,20 @@
     def xcopy(site, k, d):
         ref = xslots.at[site, px, k]
         return pltpu.make_async_remote_copy(
-            src_ref=ref, dst_ref=ref, send_sem=x_send.at[site, k, d - 1], recv_sem=x_recv.at[site, k, d - 1],
+            src_ref=ref, dst_ref=ref, send_sem=x_send.at[k, d - 1], recv_sem=x_recv.at[k, d - 1],
             device_id={"pts": lax.rem(px + d, n_x) * 2 + core}, device_id_type=MESH)
 
     def lcopy(use, i):
         ref = lslots.at[use, pl.ds(me, 1)]
         return pltpu.make_async_remote_copy(
-            src_ref=ref, dst_ref=ref, send_sem=l_send.at[use, i], recv_sem=l_recv.at[use, i],
+            src_ref=ref, dst_ref=ref, send_sem=l_send.at[use], recv_sem=l_recv.at[use],
             device_id=offset(others[i]), device_id_type=MESH)
+
+    def lwait(use):
+        ref = lslots.at[use, pl.ds(0, n_dev - 1)]
+        return pltpu.make_async_remote_copy(
+            src_ref=ref, dst_ref=ref, send_sem=l_send.at[use], recv_sem=l_recv.at[use],
+            device_id=offset(others[0]), device_id_type=MESH)
 
     def ycopy(site, d, src, dst):
         return pltpu.make_async_remote_copy(
@@ -219,9 +228,6 @@
         e[part, cols] = err
         sq[...] += jnp.sum((err * err).reshape(n_rows // 8, 8, STEP), axis=0)
 
-    def step_cols(j):
-        return pl.ds(pl.multiple_of(j * STEP, STEP), STEP)
-
     def error_rows(part):
         hi, lo = mcat[part, :rank], mcat[part, rank:]
         both = jnp.concatenate([jnp.concatenate([hi, hi], 1), jnp.concatenate([lo, lo], 1)], 0)
@@ -242,11 +248,9 @@
 
     def get_limit(use):
         with jax.named_scope("limit"):
-            for i in reversed(range(n_dev - 1)):
-                lcopy(use, i).wait_recv()
+            lwait(use).wait_recv()
         total = jnp.sum(jnp.sum(lslots[use], axis=0, keepdims=True), axis=1, keepdims=True)
-        for i in range(n_dev - 1):
-            lcopy(use, i).wait_send()
+        lwait(use).wait_send()
         return HUBER * jnp.sqrt(total / count + 1e-06)
 
     eye = (lax.broadcasted_iota(jnp.int32, (rank, rank), 0)
@@ -265,24 +269,24 @@
     sq[...] = jnp.zeros_like(sq)
     load_m.wait()
     prepare_rows(pl.ds(0, rows))
-    gram_part()
     load_c.wait()
     prepare_cols(pl.ds(0, width), c_out[...])
-    with jax.named_scope("barrier"):
-        pl.semaphore_wait(barrier, n_dev - 1)
-    start(grs)
-    for j in range(loads):
-        load_cols(j).wait()
     with jax.named_scope("err0"):
         def first(j, carry):
+            load_cols(j).wait()
             errors(pl.ds(0, rows), rows, step_cols(j))
             return carry
         lax.fori_loop(0, loads, first, 0)
+    with jax.named_scope("barrier"):
+        pl.semaphore_wait(barrier, n_dev - 1)
     send_limit(0)
+    gram_part()
+    start(grs)
 
     def outer(o, carry):
         more = o < OUTER - 1
-        finish(grs)
+        with jax.named_scope("grs"):
+            finish(grs)
         own = gpart[pl.ds(pme * gw, gw), :]
         for j in range(1, n_pts):
             own = own + gslots[j - 1]
@@ -291,20 +295,14 @@
         start(gag)
 
         for inner in range(INNER):
-            if inner == 0:
-                @pl.when(o == 0)
-                def _():
-                    finish(gag)
-                    gfull[...] = gfull[...] + eye
-                    sweep(gfull, 0, rank // PIVOTS // 2)
             limit = get_limit(inner)
 
             def give(k):
-                return ccopy(inner, k, cpart.at[k], cslots.at[inner, k])
+                return ccopy(0, k, cpart.at[k], cslots.at[inner, k])
 
             def spread(k):
                 ref = c_out.at[:, col_chunk(core, k)]
-                return ccopy(INNER + inner, k, ref, ref)
+                return ccopy(1, k, ref, ref)
 
             def products(t, carry):
                 last = t == 2 * chunks - 1
@@ -329,12 +327,10 @@
             with jax.named_scope("products"):
                 lax.fori_loop(0, 2 * chunks, products, 0)
             if inner == 0:
-                @pl.when(o > 0)
-                def _():
+                with jax.named_scope("gag"):
                     finish(gag)
-                    gfull[...] = gfull[...] + eye
-                    sweep(gfull, 0, rank // PIVOTS // 2)
-                sweep(gfull, rank // PIVOTS // 2, rank // PIVOTS // 2)
+                gfull[...] = gfull[...] + eye
+                sweep(gfull, 0, rank // PIVOTS)
 
             def update(t, carry):
                 j = t // 2
@@ -391,6 +387,9 @@
                 return carry
             lax.fori_loop(0, chunks, settle, 0)
 
+        @pl.when(jnp.logical_not(more))
+        def _():
+            c_out[...] = c_out[...] * jnp.sqrt(jnp.float32(rows * n_pts))
         with jax.named_scope("hpart"):
             hpart[...] = quads(dot(ccat[...], ctcat[...]))
             start(hrs)
@@ -501,15 +500,24 @@
             send_limit(0)
             gram_part()
             start(grs)
-        ycopy(1, 0, own_ref, own_ref).wait_send()
-        over_y(0).wait_send()
-        for d in range(1, n_z):
-            pass_on(d).wait_send()
-            over_y(d).wait_send()
-            over_z(d).wait_send()
-            zcopy(1, d, own_ref, own_ref).wait_send()
+        with jax.named_scope("sends"):
+            ycopy(1, 0, own_ref, own_ref).wait_send()
+            over_y(0).wait_send()
+            for d in range(1, n_z):
+                pass_on(d).wait_send()
+                over_y(d).wait_send()
+                over_z(d).wait_send()
+                zcopy(1, d, own_ref, own_ref).wait_send()
         return carry
     lax.fori_loop(0, OUTER, outer, 0)
+
+
+def write_out(modes, amplitudes, m_hbm, a_hbm, sem):
+    copies = [pltpu.make_async_copy(modes, m_hbm, sem.at[0]), pltpu.make_async_copy(amplitudes, a_hbm, sem.at[1])]
+    for copy in copies:
+        copy.start()
+    for copy in copies:
+        copy.wait()
 
 
 def shards(n_pts, n_snap, snapshots, modes_init, coefs_init):
@@ -517,7 +525,6 @@
     rank = modes_init.shape[1]
     rw, gw, hw = rows // n_snap, rank // n_pts, rank // n_snap
     chunks, n_x, n_z, n_dev = width // 2 // CHUNK, n_pts // 2, n_snap // 2, n_pts * n_snap
-    points = float(rows * n_pts)
     vmem, dma = pltpu.VMEM, pltpu.SemaphoreType.DMA
     scratch = [
         vmem((rows, width), F32), vmem((rows, width), F32),
@@ -534,21 +541,27 @@
         dma((2 + width // STEP,)),
         dma((2, n_pts - 1)), dma((2, n_pts - 1)),
         dma((2, n_snap - 1)), dma((2, n_snap - 1)),
-        dma((2 * INNER, chunks)), dma((2 * INNER, chunks)),
-        dma((INNER, chunks, n_x - 1)), dma((INNER, chunks, n_x - 1)),
-        dma((INNER + 1, n_dev - 1)), dma((INNER + 1, n_dev - 1)),
+        dma((2, chunks)), dma((2, chunks)),
+        dma((chunks, n_x - 1)), dma((chunks, n_x - 1)),
+        dma((INNER + 1,)), dma((INNER + 1,)),
         dma((2, n_z)), dma((2, n_z)),
         dma((2, n_z - 1)), dma((2, n_z - 1)),
     ]
     modes, coefs = pl.pallas_call(
         functools.partial(kernel, n_pts, n_snap),
-        out_shape=(jax.ShapeDtypeStruct((rows, rank), F32), jax.ShapeDtypeStruct((rank, width), F32)),
-        in_specs=[pl.BlockSpec(memory_space=pl.ANY)] * 3,
+        out_shape=(vmem((rows, rank), F32), vmem((rank, width), F32)),
+        in_specs=[pl.BlockSpec(memory_space=pltpu.HBM)] * 3,
         out_specs=(pl.BlockSpec(memory_space=vmem), pl.BlockSpec(memory_space=vmem)),
         scratch_shapes=scratch,
-        compiler_params=pltpu.CompilerParams(collective_id=0, has_side_effects=True, vmem_limit_bytes=60 * 1024 * 1024),
+        compiler_params=pltpu.CompilerParams(collective_id=0, has_side_effects=True, vmem_limit_bytes=67043328 - 5 * 256 * 1024),
     )(snapshots, modes_init, coefs_init)
-    return modes, coefs * jnp.sqrt(jnp.float32(points))
+    return pl.pallas_call(
+        write_out,
+        out_shape=(jax.ShapeDtypeStruct((rows, rank), F32), jax.ShapeDtypeStruct((rank, width), F32)),
+        in_specs=[pl.BlockSpec(memory_space=pl.ANY)] * 2,
+        out_specs=(pl.BlockSpec(memory_space=pltpu.HBM), pl.BlockSpec(memory_space=pltpu.HBM)),
+        scratch_shapes=[dma((2,))],
+    )(pltpu.with_memory_space_constraint(modes, vmem), pltpu.with_memory_space_constraint(coefs, vmem))
 
 
 def solution(mesh):

time: 131 us -> 123 us (0.939)
  Pallas kernels: 126 us -> 122 us
  other arithmetic: 1.88 us -> 0 us
  local copies, waits for them, and re-layouts: 1.87 us -> 0 us
    pallas_call x1 -> x2, Pallas kernels: 126 us -> 122 us  [the longest x1 121 us: shards(): pl.pallas_call(functools.partial(kernel, n_pts, n_snap), out_shape=(vmem(...]
    mul x1 -> x0, other arithmetic: 1.88 us -> none  [shards(): return (modes, coefs * jnp.sqrt(jnp.float32(points)))]
    unnamed x1 -> x0, local copies, waits for them, and re-layouts: 1.87 us -> none
where the time goes in v3:
time: 123 us
  Pallas kernels  122 us (99%)
    pallas_call x1, Pallas kernels, shards(): pl.pallas_call(functools.partial(kernel, n_pts, n_snap), out_shape=(vmem(...  121 us

profile of v3, /device:TPU:0, one launch (start us, length us, event | category | flops | bytes accessed | tf_op | source)
XLA Modules:
  0.0 122.9 jit_solution(2845358702651039988)
XLA Ops:
  0.6 121.3 %shard_map.50 = (f32[1024,128]{1,0:T(8,128)S(1)}, f32[128,1024]{1,0:T(8,128)S(1)}) custom-call(f32[1024,1024]{1,0:T(8,128)} %s_hbm.1, f32[1024,128]{1,0:T(8,128)} %m_hbm.1, f32[128,1024]{1,0:T(8,128)} %c_hbm.1), custom_call_target="tpu_custom_call" | custom-call | tf_op jit(solution)/shard_map/pallas_call | solution.py:550
  121.9 1.0 shard_map.51

commit v4 on v3

--- a/solution.py
+++ b/solution.py
@@ -108,23 +108,23 @@
 
     def pcopy(site, j, src, dst):
         return pltpu.make_async_remote_copy(
-            src_ref=src, dst_ref=dst, send_sem=p_send.at[site, j - 1], recv_sem=p_recv.at[site, j - 1],
+            src_ref=src, dst_ref=dst, send_sem=p_send.at[site], recv_sem=p_recv.at[site],
             device_id={"pts": pts_peer(pme, j, n_pts)}, device_id_type=MESH)
 
     def scopy(site, j, src, dst):
         return pltpu.make_async_remote_copy(
-            src_ref=src, dst_ref=dst, send_sem=s_send.at[site, j - 1], recv_sem=s_recv.at[site, j - 1],
+            src_ref=src, dst_ref=dst, send_sem=s_send.at[site], recv_sem=s_recv.at[site],
             device_id={"snap": snap_peer(sme, j, n_snap)}, device_id_type=MESH)
 
     def ccopy(site, k, src, dst):
         return pltpu.make_async_remote_copy(
-            src_ref=src, dst_ref=dst, send_sem=c_send.at[site, k], recv_sem=c_recv.at[site, k],
+            src_ref=src, dst_ref=dst, send_sem=c_send.at[site], recv_sem=c_recv.at[site, k],
             device_id={"pts": px * 2 + 1 - core}, device_id_type=MESH)
 
     def xcopy(site, k, d):
         ref = xslots.at[site, px, k]
         return pltpu.make_async_remote_copy(
-            src_ref=ref, dst_ref=ref, send_sem=x_send.at[k, d - 1], recv_sem=x_recv.at[k, d - 1],
+            src_ref=ref, dst_ref=ref, send_sem=x_send, recv_sem=x_recv.at[k, d - 1],
             device_id={"pts": lax.rem(px + d, n_x) * 2 + core}, device_id_type=MESH)
 
     def lcopy(use, i):
@@ -141,12 +141,12 @@
 
     def ycopy(site, d, src, dst):
         return pltpu.make_async_remote_copy(
-            src_ref=src, dst_ref=dst, send_sem=y_send.at[site, d], recv_sem=y_recv.at[site, d],
+            src_ref=src, dst_ref=dst, send_sem=y_send.at[site], recv_sem=y_recv.at[site, d],
             device_id={"snap": sz * 2 + 1 - sy}, device_id_type=MESH)
 
     def zcopy(site, d, src, dst):
         return pltpu.make_async_remote_copy(
-            src_ref=src, dst_ref=dst, send_sem=z_send.at[site, d - 1], recv_sem=z_recv.at[site, d - 1],
+            src_ref=src, dst_ref=dst, send_sem=z_send.at[site], recv_sem=z_recv.at[site, d - 1],
             device_id={"snap": lax.rem(sz + d, n_z) * 2 + sy}, device_id_type=MESH)
 
     def row_block(d, which):
@@ -162,11 +162,17 @@
         for copy in copies:
             copy.start()
 
-    def finish(copies):
-        for copy in copies:
-            copy.wait_recv()
-        for copy in copies:
-            copy.wait_send()
+    def all_of(ref, send_sem, recv_sem):
+        return pltpu.make_async_remote_copy(
+            src_ref=ref, dst_ref=ref, send_sem=send_sem, recv_sem=recv_sem,
+            device_id={"pts": px * 2 + 1 - core}, device_id_type=MESH)
+
+    def finish(ref, send_sem, recv_sem):
+        all_of(ref, send_sem, recv_sem).wait_recv()
+        all_of(ref, send_sem, recv_sem).wait_send()
+
+    def sent(ref, send_sem, recv_sem):
+        all_of(ref, send_sem, recv_sem).wait_send()
 
     def prepare_rows(part):
         hi, lo = split(m_out[part, :])
@@ -286,7 +292,7 @@
     def outer(o, carry):
         more = o < OUTER - 1
         with jax.named_scope("grs"):
-            finish(grs)
+            finish(gslots, p_send.at[0], p_recv.at[0])
         own = gpart[pl.ds(pme * gw, gw), :]
         for j in range(1, n_pts):
             own = own + gslots[j - 1]
@@ -328,7 +334,7 @@
                 lax.fori_loop(0, 2 * chunks, products, 0)
             if inner == 0:
                 with jax.named_scope("gag"):
-                    finish(gag)
+                    finish(gfull.at[pl.ds(0, rank - gw)], p_send.at[1], p_recv.at[1])
                 gfull[...] = gfull[...] + eye
                 sweep(gfull, 0, rank // PIVOTS)
 
@@ -379,13 +385,9 @@
                 lax.fori_loop(0, loads, update, 0)
             send_limit(inner + 1)
 
-            def settle(k, carry):
-                spread(k).wait_send()
-                give(k).wait_send()
-                for d in range(1, n_x):
-                    xcopy(inner, k, d).wait_send()
-                return carry
-            lax.fori_loop(0, chunks, settle, 0)
+            sent(cpart, c_send.at[0], c_recv.at[0, 0])
+            sent(c_out.at[:, pl.ds(0, half)], c_send.at[1], c_recv.at[1, 0])
+            sent(xslots.at[0, pl.ds(0, n_x - 1)], x_send, x_recv.at[0, 0])
 
         @pl.when(jnp.logical_not(more))
         def _():
@@ -421,7 +423,7 @@
 
             @pl.when(t == 0)
             def _():
-                finish(hrs)
+                finish(hslots, s_send.at[0], s_recv.at[0])
                 own = hpart[pl.ds(sme * hw, hw), :]
                 for j in range(1, n_snap):
                     own = own + hslots[j - 1]
@@ -431,8 +433,6 @@
             return carry
         with jax.named_scope("moments"):
             lax.fori_loop(0, 2 * n_z, moments, 0)
-        steps = rank // PIVOTS
-
         def forward(t, carry):
             d = far(t)
             with jax.named_scope("ywait"):
@@ -442,16 +442,16 @@
             @pl.when(t < n_z - 1)
             def _():
                 over_z(d).start()
-
-            @pl.when(t == 0)
-            def _():
-                with jax.named_scope("hag"):
-                    finish(hag)
-                hfull[...] = hfull[...] + eye
-            sweep(hfull, t * (steps // n_z), steps // n_z)
             return carry
-        lax.fori_loop(0, n_z, forward, 0)
-        sweep(hfull, steps // n_z * n_z, steps - steps // n_z * n_z)
+        lax.fori_loop(0, n_z - 2, forward, 0)
+        with jax.named_scope("hag"):
+            finish(hfull.at[pl.ds(0, rank - hw)], s_send.at[1], s_recv.at[1])
+        hfull[...] = hfull[...] + eye
+        early = rank // PIVOTS * 3 // 8
+        sweep(hfull, 0, early)
+        forward(n_z - 2, 0)
+        sweep(hfull, early, rank // PIVOTS - early)
+        forward(n_z - 1, 0)
         with jax.named_scope("zwait"):
             for d in range(1, n_z):
                 over_z(d).wait_recv()
@@ -462,7 +462,7 @@
         m_out[own_rows, :] = m_out[own_rows, :] - step
         own_ref = m_out.at[own_rows]
         order = [far(t) for t in range(n_z - 1)]
-        start([zcopy(1, d, own_ref, own_ref) for d in order])
+        start([zcopy(1, d, own_ref, own_ref) for d in order[1:] + order[:1]])
         ycopy(1, 0, own_ref, own_ref).start()
 
         def pass_on(d):
@@ -476,7 +476,7 @@
                 error_rows(part)
         take(own_rows)
         with jax.named_scope("gatherz"):
-            for d in order[::-1]:
+            for d in order[:0:-1] + order[:1]:
                 zcopy(1, d, own_ref, own_ref).wait_recv()
                 pass_on(d).start()
 
@@ -501,13 +501,10 @@
             gram_part()
             start(grs)
         with jax.named_scope("sends"):
-            ycopy(1, 0, own_ref, own_ref).wait_send()
-            over_y(0).wait_send()
-            for d in range(1, n_z):
-                pass_on(d).wait_send()
-                over_y(d).wait_send()
-                over_z(d).wait_send()
-                zcopy(1, d, own_ref, own_ref).wait_send()
+            sent(ypart, y_send.at[0], y_recv.at[0, 0])
+            sent(m_out.at[pl.ds(0, n_z * rw)], y_send.at[1], y_recv.at[1, 0])
+            sent(zslots, z_send.at[0], z_recv.at[0, 0])
+            sent(m_out.at[pl.ds(0, (n_z - 1) * rw)], z_send.at[1], z_recv.at[1, 0])
         return carry
     lax.fori_loop(0, OUTER, outer, 0)
 
@@ -539,13 +536,13 @@
         vmem((n_z, rw, rank), F32), vmem((n_z, rw, rank), F32),
         vmem((n_z, rw, rank), F32), vmem((n_z - 1, rw, rank), F32),
         dma((2 + width // STEP,)),
-        dma((2, n_pts - 1)), dma((2, n_pts - 1)),
-        dma((2, n_snap - 1)), dma((2, n_snap - 1)),
-        dma((2, chunks)), dma((2, chunks)),
-        dma((chunks, n_x - 1)), dma((chunks, n_x - 1)),
+        dma((2,)), dma((2,)),
+        dma((2,)), dma((2,)),
+        dma((2,)), dma((2, chunks)),
+        dma, dma((chunks, n_x - 1)),
         dma((INNER + 1,)), dma((INNER + 1,)),
-        dma((2, n_z)), dma((2, n_z)),
-        dma((2, n_z - 1)), dma((2, n_z - 1)),
+        dma((2,)), dma((2, n_z)),
+        dma((2,)), dma((2, n_z - 1)),
     ]
     modes, coefs = pl.pallas_call(
         functools.partial(kernel, n_pts, n_snap),

time: 123 us -> 121 us (0.984)
  Pallas kernels: 122 us -> 120 us
    pallas_call x1, Pallas kernels: 121 us -> 119 us  [shards(): pl.pallas_call(functools.partial(kernel, n_pts, n_snap), out_shape=(vmem(...]
where the time goes in v4:
time: 121 us; the launch traced here: 120 us
  Pallas kernels  120 us (99%)
    pallas_call x1, Pallas kernels, shards(): pl.pallas_call(functools.partial(kernel, n_pts, n_snap), out_shape=(vmem(...  119 us

profile of v4, /device:TPU:0, one launch (start us, length us, event | category | flops | bytes accessed | tf_op | source)
XLA Modules:
  0.0 120.5 jit_solution(7576336581588293915)
XLA Ops:
  0.6 118.8 %shard_map.50 = (f32[1024,128]{1,0:T(8,128)S(1)}, f32[128,1024]{1,0:T(8,128)S(1)}) custom-call(f32[1024,1024]{1,0:T(8,128)} %s_hbm.1, f32[1024,128]{1,0:T(8,128)} %m_hbm.1, f32[128,1024]{1,0:T(8,128)} %c_hbm.1), custom_call_target="tpu_custom_call" | custom-call | tf_op jit(solution)/shard_map/pallas_call | solution.py:547
  119.5 1.0 shard_map.51

commit v5 on v4

--- a/solution.py
+++ b/solution.py
@@ -68,6 +68,7 @@
     n_dev = n_pts * n_snap
     me = pme * n_snap + sme
     rw = rows // n_snap
+    rh = rw // 2
     half = width // 2
     chunks = half // CHUNK
     n_x, n_z = n_pts // 2, n_snap // 2
@@ -139,21 +140,30 @@
             src_ref=ref, dst_ref=ref, send_sem=l_send.at[use], recv_sem=l_recv.at[use],
             device_id=offset(others[0]), device_id_type=MESH)
 
-    def ycopy(site, d, src, dst):
-        return pltpu.make_async_remote_copy(
-            src_ref=src, dst_ref=dst, send_sem=y_send.at[site], recv_sem=y_recv.at[site, d],
+    def half_of(ref, h):
+        return ref.at[pl.ds(pl.multiple_of(h * rh, rh), rh)]
+
+    def ycopy(site, d, h, src, dst):
+        return pltpu.make_async_remote_copy(
+            src_ref=src, dst_ref=dst, send_sem=y_send.at[site], recv_sem=y_recv.at[site, d, h],
             device_id={"snap": sz * 2 + 1 - sy}, device_id_type=MESH)
 
-    def zcopy(site, d, src, dst):
-        return pltpu.make_async_remote_copy(
-            src_ref=src, dst_ref=dst, send_sem=z_send.at[site], recv_sem=z_recv.at[site, d - 1],
-            device_id={"snap": lax.rem(sz + d, n_z) * 2 + sy}, device_id_type=MESH)
-
-    def row_block(d, which):
-        return pl.ds(pl.multiple_of((lax.rem(sz + d, n_z) * 2 + which) * rw, rw), rw)
+    def zcopy(site, d, h, src, dst):
+        return pltpu.make_async_remote_copy(
+            src_ref=src, dst_ref=dst, send_sem=z_send.at[site], recv_sem=z_recv.at[site, d - 1, h],
+            device_id={"snap": z_peer(d) * 2 + sy}, device_id_type=MESH)
+
+    def z_peer(d):
+        return (sz // 2 + d // 2) % (n_z // 2) * 2 + (sz + d) % 2
+
+    def z_from(d):
+        return (sz // 2 + n_z // 2 - d // 2) % (n_z // 2) * 2 + (sz + d) % 2
+
+    def row_block(z, which):
+        return pl.ds(pl.multiple_of((z * 2 + which) * rw, rw), rw)
 
     def far(t):
-        return n_z // 2 + ((t + 1) // 2) * (1 - 2 * (t % 2))
+        return n_z - 1 - t
 
     def col_chunk(which, k):
         return pl.ds(pl.multiple_of(which * half + k * CHUNK, CHUNK), CHUNK)
@@ -401,25 +411,29 @@
             hi, lo = split(jnp.clip(e[part, :], -limit, limit))
             return quads(dot(jnp.concatenate([hi, lo], 0), ctcat[...]))
 
-        def over_y(d):
-            return ycopy(0, d, ypart.at[d], yslots.at[d])
-
-        def over_z(d):
-            return zcopy(0, d, zpart.at[d], zslots.at[d - 1])
+        def over_y(d, h):
+            return ycopy(0, d, h, half_of(ypart.at[d], h), half_of(yslots.at[d], h))
+
+        def over_z(d, h):
+            return zcopy(0, d, h, half_of(zpart.at[d], h), half_of(zslots.at[d - 1], h))
 
         def moments(t, carry):
             theirs = t < n_z
             d = far(t % n_z)
-            value = moment(row_block(d, jnp.where(theirs, 1 - sy, sy)))
+            value = moment(row_block(z_peer(d), jnp.where(theirs, 1 - sy, sy)))
 
             @pl.when(theirs)
             def _():
                 ypart[d] = value
-                over_y(d).start()
+                over_y(d, 0).start()
 
             @pl.when(jnp.logical_not(theirs))
             def _():
                 zpart[d] = value
+
+            @pl.when(t == n_z - 1)
+            def _():
+                start([over_y(far(u), 1) for u in range(n_z)])
 
             @pl.when(t == 0)
             def _():
@@ -434,40 +448,55 @@
         with jax.named_scope("moments"):
             lax.fori_loop(0, 2 * n_z, moments, 0)
         def forward(t, carry):
-            d = far(t)
+            d, h = far(t % n_z), t // n_z
+            part = pl.ds(pl.multiple_of(h * rh, rh), rh)
             with jax.named_scope("ywait"):
-                over_y(d).wait_recv()
-            zpart[d] = zpart[d] + yslots[d]
-
-            @pl.when(t < n_z - 1)
+                over_y(d, h).wait_recv()
+            zpart[d, part, :] = zpart[d, part, :] + yslots[d, part, :]
+
+            @pl.when(d > 0)
             def _():
-                over_z(d).start()
-            return carry
-        lax.fori_loop(0, n_z - 2, forward, 0)
+                over_z(d, h).start()
+            return carry
+        lax.fori_loop(0, n_z, forward, 0)
         with jax.named_scope("hag"):
             finish(hfull.at[pl.ds(0, rank - hw)], s_send.at[1], s_recv.at[1])
         hfull[...] = hfull[...] + eye
-        early = rank // PIVOTS * 3 // 8
-        sweep(hfull, 0, early)
-        forward(n_z - 2, 0)
-        sweep(hfull, early, rank // PIVOTS - early)
-        forward(n_z - 1, 0)
-        with jax.named_scope("zwait"):
+        steps = rank // PIVOTS
+        per = steps // n_z
+
+        def sweep_forward(t, carry):
+            sweep(hfull, t * per, per)
+            return forward(n_z + t, carry)
+        lax.fori_loop(0, n_z, sweep_forward, 0)
+        sweep(hfull, per * n_z, steps - per * n_z)
+
+        def modes_half(z, which, h):
+            return m_out.at[pl.ds(pl.multiple_of((z * 2 + which) * rw + h * rh, rh), rh)]
+
+        def gather(d, h):
+            ref = modes_half(sz, sy, h)
+            return zcopy(1, d, h, ref, ref)
+
+        def pass_on(d, h):
+            ref = modes_half(z_from(d), sy, h)
+            return ycopy(1, d, h, ref, ref)
+
+        def solve(h, carry):
+            with jax.named_scope("zwait"):
+                for d in range(1, n_z):
+                    over_z(d, h).wait_recv()
+            part = pl.ds(pl.multiple_of(h * rh, rh), rh)
+            share = zpart[0, part, :]
             for d in range(1, n_z):
-                over_z(d).wait_recv()
-        share = zpart[0]
-        for d in range(1, n_z):
-            share = share + zslots[d - 1]
-        step = jnp.dot(share, hfull[...], preferred_element_type=F32, precision=lax.Precision.HIGHEST)
-        m_out[own_rows, :] = m_out[own_rows, :] - step
-        own_ref = m_out.at[own_rows]
-        order = [far(t) for t in range(n_z - 1)]
-        start([zcopy(1, d, own_ref, own_ref) for d in order[1:] + order[:1]])
-        ycopy(1, 0, own_ref, own_ref).start()
-
-        def pass_on(d):
-            ref = m_out.at[row_block(n_z - d, sy)]
-            return ycopy(1, d, ref, ref)
+                share = share + zslots[d - 1, part, :]
+            step = jnp.dot(share, hfull[...], preferred_element_type=F32, precision=lax.Precision.HIGHEST)
+            mine = pl.ds(pl.multiple_of(sme * rw + h * rh, rh), rh)
+            m_out[mine, :] = m_out[mine, :] - step
+            start([gather(far(t), h) for t in range(n_z - 1)])
+            pass_on(0, h).start()
+            return carry
+        lax.fori_loop(0, 2, solve, 0)
 
         def take(part):
             @pl.when(more)
@@ -475,22 +504,31 @@
                 prepare_rows(part)
                 error_rows(part)
         take(own_rows)
-        with jax.named_scope("gatherz"):
-            for d in order[:0:-1] + order[:1]:
-                zcopy(1, d, own_ref, own_ref).wait_recv()
-                pass_on(d).start()
-
-        def near(u, carry):
-            take(row_block(u, sy))
-            return carry
-        with jax.named_scope("near"):
-            lax.fori_loop(1, n_z, near, 0)
+
+        def near(u):
+            return jnp.where(u == 0, 1, n_z - u)
+
+        def first_half(u, carry):
+            with jax.named_scope("gatherz"):
+                gather(near(u), 0).wait_recv()
+            pass_on(near(u), 0).start()
+            return carry
+        lax.fori_loop(0, n_z - 1, first_half, 0)
+
+        def second_half(u, carry):
+            with jax.named_scope("gatherz"):
+                gather(near(u), 1).wait_recv()
+            pass_on(near(u), 1).start()
+            take(row_block(z_from(near(u)), sy))
+            return carry
+        lax.fori_loop(0, n_z - 1, second_half, 0)
 
         def other(u, carry):
-            d = jnp.where(u == 0, 0, far(n_z - 1 - u))
+            d = jnp.where(u == 0, 0, near(u - 1))
             with jax.named_scope("gathery"):
-                pass_on(d).wait_recv()
-            take(row_block(n_z - d, 1 - sy))
+                pass_on(d, 0).wait_recv()
+                pass_on(d, 1).wait_recv()
+            take(row_block(z_from(d), 1 - sy))
             return carry
         with jax.named_scope("other"):
             lax.fori_loop(0, n_z, other, 0)
@@ -501,10 +539,10 @@
             gram_part()
             start(grs)
         with jax.named_scope("sends"):
-            sent(ypart, y_send.at[0], y_recv.at[0, 0])
-            sent(m_out.at[pl.ds(0, n_z * rw)], y_send.at[1], y_recv.at[1, 0])
-            sent(zslots, z_send.at[0], z_recv.at[0, 0])
-            sent(m_out.at[pl.ds(0, (n_z - 1) * rw)], z_send.at[1], z_recv.at[1, 0])
+            sent(ypart, y_send.at[0], y_recv.at[0, 0, 0])
+            sent(m_out.at[pl.ds(0, n_z * rw)], y_send.at[1], y_recv.at[1, 0, 0])
+            sent(zslots, z_send.at[0], z_recv.at[0, 0, 0])
+            sent(m_out.at[pl.ds(0, (n_z - 1) * rw)], z_send.at[1], z_recv.at[1, 0, 0])
         return carry
     lax.fori_loop(0, OUTER, outer, 0)
 
@@ -541,8 +579,8 @@
         dma((2,)), dma((2, chunks)),
         dma, dma((chunks, n_x - 1)),
         dma((INNER + 1,)), dma((INNER + 1,)),
-        dma((2,)), dma((2, n_z)),
-        dma((2,)), dma((2, n_z - 1)),
+        dma((2,)), dma((2, n_z, 2)),
+        dma((2,)), dma((2, n_z - 1, 2)),
     ]
     modes, coefs = pl.pallas_call(
         functools.partial(kernel, n_pts, n_snap),

time: 121 us -> 119 us (0.983)
  Pallas kernels: 120 us -> 118 us
    pallas_call x1, Pallas kernels: 119 us -> 117 us  [shards(): pl.pallas_call(functools.partial(kernel, n_pts, n_snap), out_shape=(vmem(...]
where the time goes in v5:
time: 119 us
  Pallas kernels  118 us (99%)
    pallas_call x1, Pallas kernels, shards(): pl.pallas_call(functools.partial(kernel, n_pts, n_snap), out_shape=(vmem(...  117 us

profile of v5, /device:TPU:0, one launch (start us, length us, event | category | flops | bytes accessed | tf_op | source)
XLA Modules:
  0.0 119.0 jit_solution(15612340738312647019)
XLA Ops:
  0.6 117.3 %shard_map.50 = (f32[1024,128]{1,0:T(8,128)S(1)}, f32[128,1024]{1,0:T(8,128)S(1)}) custom-call(f32[1024,1024]{1,0:T(8,128)} %s_hbm.1, f32[1024,128]{1,0:T(8,128)} %m_hbm.1, f32[128,1024]{1,0:T(8,128)} %c_hbm.1), custom_call_target="tpu_custom_call" | custom-call | tf_op jit(solution)/shard_map/pallas_call | solution.py:585
  118.0 1.0 shard_map.51

commit v6 on v5

--- a/solution.py
+++ b/solution.py
@@ -199,11 +199,6 @@
         ccat[:rank, cols] = hi
         ccat[rank:, cols] = lo
 
-    def prepare_ct(cols, value):
-        hi, lo = split(value.T)
-        ctcat[cols, :rank] = hi
-        ctcat[cols, rank:] = lo
-
     def sweep(ref, base, steps):
         sub = lax.broadcasted_iota(jnp.int32, (PIVOTS, rank), 0)
         lane = lax.broadcasted_iota(jnp.int32, (PIVOTS, rank), 1)
@@ -236,13 +231,13 @@
         with jax.named_scope("sweep"):
             lax.fori_loop(0, steps, body, 0)
 
-    def errors(part, n_rows, cols):
+    def errors(part, n_rows, cols, n_cols=STEP):
         hi, lo = mcat[part, :rank], mcat[part, rank:]
         c = ccat[:, cols]
         fit = dot(jnp.concatenate([hi, hi], 1), c) + dot(jnp.concatenate([lo, lo], 1), c)
         err = s[part, cols] - fit
         e[part, cols] = err
-        sq[...] += jnp.sum((err * err).reshape(n_rows // 8, 8, STEP), axis=0)
+        sq[:, :n_cols] += jnp.sum((err * err).reshape(n_rows // 8, 8, n_cols), axis=0)
 
     def error_rows(part):
         hi, lo = mcat[part, :rank], mcat[part, rank:]
@@ -366,18 +361,15 @@
                     c_out[:, cols] = value
                     spread(k).start()
                     prepare_cols(cols, value)
-                    if inner == INNER - 1:
-                        prepare_ct(cols, value)
                     return carry
 
                 def their_cols(i, carry):
                     k = j * per + i
                     spread(k).wait_recv()
                     cols = col_chunk(1 - core, k)
-                    value = c_out[:, cols]
-                    prepare_cols(cols, value)
-                    if inner == INNER - 1:
-                        prepare_ct(cols, value)
+                    prepare_cols(cols, c_out[:, cols])
+                    if inner:
+                        errors(pl.ds(0, rows), rows, cols, CHUNK)
                     return carry
 
                 @pl.when(mine)
@@ -388,7 +380,9 @@
                 def _():
                     lax.fori_loop(0, per, their_cols, 0)
                 which = jnp.where(mine, core, 1 - core)
-                with jax.named_scope("errchunk"):
+
+                @pl.when(mine | (inner == 0))
+                def _():
                     errors(pl.ds(0, rows), rows, pl.ds(pl.multiple_of(which * half + j * STEP, STEP), STEP))
                 return carry
             with jax.named_scope("update"):
@@ -399,12 +393,16 @@
             sent(c_out.at[:, pl.ds(0, half)], c_send.at[1], c_recv.at[1, 0])
             sent(xslots.at[0, pl.ds(0, n_x - 1)], x_send, x_recv.at[0, 0])
 
+        with jax.named_scope("hpart"):
+            hi, lo = split(c_out[...].T)
+            ctcat[:, :rank] = hi
+            ctcat[:, rank:] = lo
+            hpart[...] = quads(dot(ccat[...], ctcat[...]))
+            start(hrs)
+
         @pl.when(jnp.logical_not(more))
         def _():
             c_out[...] = c_out[...] * jnp.sqrt(jnp.float32(rows * n_pts))
-        with jax.named_scope("hpart"):
-            hpart[...] = quads(dot(ccat[...], ctcat[...]))
-            start(hrs)
         limit = get_limit(INNER)
 
         def moment(part):

time: 119 us -> 119 us (level)
  no operation moved by 1% of the time
where the time goes in v6:
time: 119 us
  Pallas kernels  118 us (99%)
    pallas_call x1, Pallas kernels, shards(): pl.pallas_call(functools.partial(kernel, n_pts, n_snap), out_shape=(vmem(...  117 us

profile of v6, /device:TPU:0, one launch (start us, length us, event | category | flops | bytes accessed | tf_op | source)
XLA Modules:
  0.0 118.8 jit_solution(2967637253410813414)
XLA Ops:
  0.6 117.2 %shard_map.50 = (f32[1024,128]{1,0:T(8,128)S(1)}, f32[128,1024]{1,0:T(8,128)S(1)}) custom-call(f32[1024,1024]{1,0:T(8,128)} %s_hbm.1, f32[1024,128]{1,0:T(8,128)} %m_hbm.1, f32[128,1024]{1,0:T(8,128)} %c_hbm.1), custom_call_target="tpu_custom_call" | custom-call | tf_op jit(solution)/shard_map/pallas_call | solution.py:583
  117.8 1.0 shard_map.51

commit v7 on v6

v7 whole, which is shorter than its diff:
```python
import functools

import jax
import jax.numpy as jnp
from jax import lax
from jax.experimental import pallas as pl
from jax.experimental.pallas import tpu as pltpu
from jax.sharding import PartitionSpec as P

OUTER = 2
INNER = 2
PIVOTS = 16
CHUNK = 128
STEP = 256
LAG = 2

HUBER = 1.345
RIDGE = 0.01

F32 = jnp.float32
BF16 = jnp.bfloat16
MESH = pl.DeviceIdType.MESH


def split(x):
    hi = x.astype(BF16)
    lo = (x - hi.astype(F32)).astype(BF16)
    return hi, lo


def split3(x):
    hi = x.astype(BF16)
    rest = x - hi.astype(F32)
    mid = rest.astype(BF16)
    lo = (rest - mid.astype(F32)).astype(BF16)
    return hi, mid, lo


def dot(a, b):
    return jnp.dot(a, b, preferred_element_type=F32)


def quads(x):
    r, c = x.shape[0] // 2, x.shape[1] // 2
    return (x[:r, :c] + x[:r, c:]) + (x[r:, :c] + x[r:, c:])


def kernel(n_pts, n_snap, s_hbm, m_hbm, c_hbm, m_out, c_out,
           s, e, s_far, e_far, m_far, c_now, c_far, mcat, mtcat, ccat, ccat_far, ctcat, sq,
           gslots, gfull, hpart, hslots, hred, hfull,
           lslots, xslots, opart, oslots, ypart, yslots, zpart, zslots,
           load_sem, g_send, g_recv, h_send, h_recv, c_send, c_recv, x_send, x_recv,
           l_send, l_recv, y_send, y_recv, z_send, z_recv):
    rows, rank = m_out.shape
    width = c_out.shape[1]
    pme = lax.axis_index("pts")
    sme = lax.axis_index("snap")
    n_dev = n_pts * n_snap
    me = pme * n_snap + sme
    rw = rows // n_snap
    rh = rw // 2
    half = width // 2
    chunks = half // CHUNK
    n_x, n_z = n_pts // 2, n_snap // 2
    px, core = pme // 2, lax.rem(pme, 2)
    sz, sy = sme // 2, lax.rem(sme, 2)
    group = 2 * n_snap
    gme = core * n_snap + sme
    hw = rank // group
    count = float(rows * n_pts * width * n_snap)
    loads = half // STEP
    whole = pl.ds(0, 2 * rows)
    own_points = pl.ds(pl.multiple_of(core * rows, rows), rows)
    far_points = pl.ds(pl.multiple_of((1 - core) * rows, rows), rows)

    def offset(d):
        dx, dc, dz, dy = d
        return {"pts": lax.rem(px + dx, n_x) * 2 + lax.rem(core + dc, 2),
                "snap": lax.rem(sz + dz, n_z) * 2 + lax.rem(sy + dy, 2)}

    def hops(d):
        dx, dc, dz, dy = d
        return min(dx, n_x - dx) + dy + min(dz, n_z - dz) + 0.1 * dc
    others = [(dx, dc, dz, dy) for dx in range(n_x) for dc in range(2) for dz in range(n_z) for dy in range(2)][1:]
    others.sort(key=lambda d: -hops(d))

    barrier = pltpu.get_barrier_semaphore()
    for d in others:
        pl.semaphore_signal(barrier, inc=1, device_id=offset(d), device_id_type=MESH)

    def step_cols(j):
        return pl.ds(pl.multiple_of(j * STEP, STEP), STEP)

    def snap_cols(which, j):
        return pl.ds(pl.multiple_of(which * half + j * STEP, STEP), STEP)

    def load_own(j):
        return pltpu.make_async_copy(
            s_hbm.at[:, snap_cols(core, j)], s.at[own_points, step_cols(j)], load_sem.at[3 + j])

    def load_far(j):
        return pltpu.make_async_copy(
            s_hbm.at[:, snap_cols(1 - core, j)], s_far.at[:, step_cols(j)], load_sem.at[3 + loads + j])

    def side(which):
        return pl.ds(pl.multiple_of(which * half, half), half)
    load_m = pltpu.make_async_copy(m_hbm, m_out, load_sem.at[0])
    load_c = pltpu.make_async_copy(c_hbm.at[:, side(core)], c_now, load_sem.at[1])
    load_c_far = pltpu.make_async_copy(c_hbm.at[:, side(1 - core)], c_far, load_sem.at[2])
    start_all = [load_m, load_c] + [load_own(j) for j in range(loads)] + [load_c_far] + [load_far(j) for j in range(loads)]
    for copy in start_all:
        copy.start()

    def gcopy(d):
        ref = gslots.at[px]
        return pltpu.make_async_remote_copy(
            src_ref=ref, dst_ref=ref, send_sem=g_send, recv_sem=g_recv.at[d - 1],
            device_id={"pts": lax.rem(px + d, n_x) * 2 + core}, device_id_type=MESH)

    def hcopy(site, j, src, dst):
        peer = lax.rem(gme + j, group)
        return pltpu.make_async_remote_copy(
            src_ref=src, dst_ref=dst, send_sem=h_send.at[site], recv_sem=h_recv.at[site],
            device_id={"pts": px * 2 + peer // n_snap, "snap": lax.rem(peer, n_snap)}, device_id_type=MESH)

    def h_rows(g):
        return pl.ds(pl.multiple_of(g * hw, hw), hw)

    def ccopy(site, k, src, dst):
        return pltpu.make_async_remote_copy(
            src_ref=src, dst_ref=dst, send_sem=c_send.at[site + k if site == 2 else site], recv_sem=c_recv.at[min(site, 3), k],
            device_id={"pts": px * 2 + 1 - core}, device_id_type=MESH)

    def xcopy(site, k, d):
        ref = xslots.at[site, px, k]
        return pltpu.make_async_remote_copy(
            src_ref=ref, dst_ref=ref, send_sem=x_send, recv_sem=x_recv.at[k, d - 1],
            device_id={"pts": lax.rem(px + d, n_x) * 2 + core}, device_id_type=MESH)

    def lcopy(use, i):
        ref = lslots.at[use, pl.ds(me, 1)]
        return pltpu.make_async_remote_copy(
            src_ref=ref, dst_ref=ref, send_sem=l_send.at[use], recv_sem=l_recv.at[use],
            device_id=offset(others[i]), device_id_type=MESH)

    def lwait(use):
        ref = lslots.at[use, pl.ds(0, n_dev - 1)]
        return pltpu.make_async_remote_copy(
            src_ref=ref, dst_ref=ref, send_sem=l_send.at[use], recv_sem=l_recv.at[use],
            device_id=offset(others[0]), device_id_type=MESH)

    def half_of(ref, h):
        return ref.at[pl.ds(pl.multiple_of(h * rh, rh), rh)]

    def ycopy(site, d, h, src, dst):
        return pltpu.make_async_remote_copy(
            src_ref=src, dst_ref=dst, send_sem=y_send.at[site], recv_sem=y_recv.at[site, d, h],
            device_id={"snap": sz * 2 + 1 - sy}, device_id_type=MESH)

    def zcopy(site, d, h, src, dst):
        return pltpu.make_async_remote_copy(
            src_ref=src, dst_ref=dst, send_sem=z_send.at[site], recv_sem=z_recv.at[site, d - 1, h],
            device_id={"snap": z_peer(d) * 2 + sy}, device_id_type=MESH)

    def z_peer(d):
        return (sz // 2 + d // 2) % (n_z // 2) * 2 + (sz + d) % 2

    def z_from(d):
        return (sz // 2 + n_z // 2 - d // 2) % (n_z // 2) * 2 + (sz + d) % 2

    def row_block(z, which):
        return (z * 2 + which) * rw

    def far(t):
        return n_z - 1 - t

    def start(copies):
        for copy in copies:
            copy.start()

    def all_of(ref, send_sem, recv_sem):
        return pltpu.make_async_remote_copy(
            src_ref=ref, dst_ref=ref, send_sem=send_sem, recv_sem=recv_sem,
            device_id={"pts": px * 2 + 1 - core}, device_id_type=MESH)

    def finish(ref, send_sem, recv_sem):
        all_of(ref, send_sem, recv_sem).wait_recv()
        all_of(ref, send_sem, recv_sem).wait_send()

    def sent(ref, send_sem, recv_sem):
        all_of(ref, send_sem, recv_sem).wait_send()

    def prepare_rows(part, value):
        hi, lo = split(value)
        mcat[part, :rank] = hi
        mcat[part, rank:] = lo

    def prepare_mt():
        for ref, part in ((m_out, own_points), (m_far, far_points)):
            hi, lo = split(ref[...].T)
            mtcat[:rank, part] = hi
            mtcat[rank:, part] = lo

    def prepare_cols(ref, cols, value):
        hi, lo = split(value)
        ref[:rank, cols] = hi
        ref[rank:, cols] = lo

    def sweep(ref, base, steps):
        sub = lax.broadcasted_iota(jnp.int32, (PIVOTS, rank), 0)
        lane = lax.broadcasted_iota(jnp.int32, (PIVOTS, rank), 1)
        wide = lax.broadcasted_iota(jnp.int32, (rank, rank), 1)
        side = sub[:, :1]

        def body(t, carry):
            k = (base + t) * PIVOTS
            rws = pl.ds(pl.multiple_of(k, PIVOTS), PIVOTS)
            before = ref[rws, :]
            after = before
            cols = [jnp.sum(jnp.where(lane == k + p, before, 0.0), axis=1, keepdims=True) for p in range(PIVOTS)]
            for p in range(PIVOTS):
                col = cols[p]
                inv = 1.0 / col[p:p + 1, :]
                row = after[p:p + 1, :] * inv
                for q in range(p + 1, PIVOTS):
                    f = cols[q][p:p + 1, :] * inv
                    cols[q] = jnp.where(side == p, f, cols[q] - col * f)
                after = jnp.where(lane == k + p, col * inv, after - col * row)
                after = jnp.where(sub == p, jnp.where(lane == k + p, -inv, row), after)
            h, m, l = split3(before)
            a, b, c = split3(after)
            change = lax.dot_general(
                jnp.concatenate([h, h, m, h, m, l], 0), jnp.concatenate([a, b, a, c, b, a], 0),
                (((0,), (0,)), ((), ())), preferred_element_type=F32)
            ref[...] = jnp.where((wide >= k) & (wide < k + PIVOTS), 0.0, ref[...]) - change
            ref[rws, :] = after
            return carry
        with jax.named_scope("sweep"):
            lax.fori_loop(0, steps, body, 0)

    def errors(src, dst, part, m_part, n_rows, c_ref, cols, n_cols):
        c = jnp.concatenate([c_ref[:rank, cols], c_ref[rank:, cols]], 1)
        fit = dot(mcat[m_part, :], jnp.concatenate([c, c], 0))
        err = src[part, cols] - (fit[:, :n_cols] + fit[:, n_cols:])
        dst[part, cols] = err
        sq[:, :n_cols] += jnp.sum((err * err).reshape(n_rows // 8, 8, n_cols), axis=0)

    def error_rows(part):
        hi, lo = mcat[part, :rank], mcat[part, rank:]
        both = jnp.concatenate([jnp.concatenate([hi, hi], 1), jnp.concatenate([lo, lo], 1)], 0)
        for j in range(loads):
            cols = pl.ds(j * STEP, STEP)
            fit = dot(both, ccat[:, cols])
            err = s[part, cols] - (fit[:rw] + fit[rw:])
            e[part, cols] = err
            sq[...] += jnp.sum((err * err).reshape(rw // 8, 8, STEP), axis=0)

    def send_limit(use):
        acc = sq[:, :128]
        for k in range(1, STEP // 128):
            acc = acc + sq[:, k * 128:(k + 1) * 128]
        lslots[use, pl.ds(me, 1), :] = jnp.sum(acc, axis=0, keepdims=True)
        start([lcopy(use, i) for i in range(n_dev - 1)])
        sq[...] = jnp.zeros_like(sq)

    def get_limit(use):
        with jax.named_scope("limit"):
            lwait(use).wait_recv()
        total = jnp.sum(jnp.sum(lslots[use], axis=0, keepdims=True), axis=1, keepdims=True)
        lwait(use).wait_send()
        return HUBER * jnp.sqrt(total / count + 1e-06)

    eye = (lax.broadcasted_iota(jnp.int32, (rank, rank), 0)
           == lax.broadcasted_iota(jnp.int32, (rank, rank), 1)).astype(F32) * RIDGE

    hrs = [hcopy(0, j, hpart.at[h_rows(lax.rem(gme + j, group))], hslots.at[j - 1]) for j in range(1, group)]
    hag = [hcopy(1, j, hred, hfull.at[h_rows(gme)]) for j in range(1, group)]

    def gram_part():
        prepare_mt()
        gslots[px] = quads(dot(mtcat[...], mcat[...]))
        start([gcopy(d) for d in range(1, n_x)])

    sq[...] = jnp.zeros_like(sq)
    load_m.wait()
    prepare_rows(own_points, m_out[...])
    load_c.wait()
    prepare_cols(ccat, pl.ds(0, half), c_now[...])
    with jax.named_scope("err0"):
        def first_own(j, carry):
            load_own(j).wait()
            errors(s, e, own_points, own_points, rows, ccat, step_cols(j), STEP)
            return carry
        lax.fori_loop(0, loads, first_own, 0)
        load_c_far.wait()
        prepare_cols(ccat_far, pl.ds(0, half), c_far[...])

        def first_far(j, carry):
            load_far(j).wait()
            errors(s_far, e_far, pl.ds(0, rows), own_points, rows, ccat_far, step_cols(j), STEP)
            return carry
        lax.fori_loop(0, loads, first_far, 0)
    with jax.named_scope("barrier"):
        pl.semaphore_wait(barrier, n_dev - 1)
    send_limit(0)
    swap = [ccopy(2, 0, m_out, m_far), ccopy(2, 1, e_far, e.at[own_points]), ccopy(2, 2, s_far, s.at[own_points])]
    start(swap)
    with jax.named_scope("mswap"):
        swap[0].wait_recv()
    prepare_rows(far_points, m_far[...])
    gram_part()

    amplitudes = ccopy(5, 0, c_out.at[:, side(core)], c_out.at[:, side(core)])

    def outer(o, carry):
        more = o < OUTER - 1

        for inner in range(INNER):
            limit = get_limit(inner)

            if inner == 0:
                @pl.when(o == 0)
                def _():
                    with jax.named_scope("eswap"):
                        swap[1].wait_recv()

            def products(k, carry):
                cols = pl.ds(pl.multiple_of(k * CHUNK, CHUNK), CHUNK)
                hi, lo = split(jnp.clip(e[:, cols], -limit, limit))
                xslots[inner, px, k] = quads(dot(mtcat[...], jnp.concatenate([hi, lo], 1)))
                for d in range(1, n_x):
                    xcopy(inner, k, d).start()
                return carry
            with jax.named_scope("products"):
                lax.fori_loop(0, chunks, products, 0)
            if inner == 0:
                with jax.named_scope("gwait"):
                    for d in range(1, n_x):
                        gcopy(d).wait_recv()
                total = gslots[0]
                for x in range(1, n_x):
                    total = total + gslots[x]
                gfull[...] = total + eye
                sent(gslots.at[pl.ds(0, n_x - 1)], g_send, g_recv.at[0])
                sweep(gfull, 0, rank // PIVOTS)

                @pl.when(o == 0)
                def _():
                    with jax.named_scope("sswap"):
                        swap[2].wait_recv()
                    sent(m_out, c_send.at[2], c_recv.at[2, 0])
                    sent(e_far, c_send.at[3], c_recv.at[2, 1])
                    sent(s_far, c_send.at[4], c_recv.at[2, 2])
            wide = CHUNK

            def update(j, carry):
                def own_cols(i, carry):
                    k = j * (wide // CHUNK) + i
                    with jax.named_scope("xw"):
                        for d in range(1, n_x):
                            xcopy(inner, k, d).wait_recv()
                    share = xslots[inner, 0, k]
                    for x in range(1, n_x):
                        share = share + xslots[inner, x, k]
                    step = jnp.dot(gfull[...], share, preferred_element_type=F32, precision=lax.Precision.HIGHEST)
                    cols = pl.ds(pl.multiple_of(k * CHUNK, CHUNK), CHUNK)
                    value = c_now[:, cols] - step
                    c_now[:, cols] = value
                    prepare_cols(ccat, cols, value)
                    return carry
                lax.fori_loop(0, wide // CHUNK, own_cols, 0)
                errors(s, e, whole, whole, 2 * rows, ccat, pl.ds(pl.multiple_of(j * wide, wide), wide), wide)
                return carry
            with jax.named_scope("update"):
                lax.fori_loop(0, half // wide, update, 0)
            send_limit(inner + 1)

            sent(xslots.at[0, pl.ds(0, n_x - 1)], x_send, x_recv.at[0, 0])

        with jax.named_scope("hpart"):
            hi, lo = split(c_now[...].T)
            ctcat[:, :rank] = hi
            ctcat[:, rank:] = lo
            hpart[...] = quads(dot(ccat[...], ctcat[...]))
            start(hrs)

        @pl.when(jnp.logical_not(more))
        def _():
            c_out[:, side(core)] = c_now[...] * jnp.sqrt(jnp.float32(rows * n_pts))
            amplitudes.start()
        limit = get_limit(INNER)

        def moment(block):
            parts = []
            for q in (1 - core, core):
                part = pl.ds(pl.multiple_of(q * rows + block, rw), rw)
                parts += split(jnp.clip(e[part, :], -limit, limit))
            both = dot(jnp.concatenate(parts, 0), ctcat[...])
            return quads(both[:2 * rw]), quads(both[2 * rw:])

        def over_y(d, h):
            return ycopy(0, d, h, half_of(ypart.at[d], h), half_of(yslots.at[d], h))

        def over_z(d, h):
            return zcopy(0, d, h, half_of(zpart.at[d], h), half_of(zslots.at[d - 1], h))

        def across(t):
            return ccopy(0, t, opart.at[t], oslots.at[t])

        def moments(t, carry):
            @pl.when(t < 2 * n_z)
            def _():
                theirs = t < n_z
                block = row_block(z_peer(far(t % n_z)), jnp.where(theirs, 1 - sy, sy))
                opart[t], value = moment(block)
                across(t).start()

                @pl.when(theirs)
                def _():
                    ypart[far(t % n_z)] = value

                @pl.when(jnp.logical_not(theirs))
                def _():
                    zpart[far(t % n_z)] = value

            @pl.when(t == 1)
            def _():
                finish(hslots, h_send.at[0], h_recv.at[0])
                own = hpart[h_rows(gme), :]
                for j in range(1, group):
                    own = own + hslots[j - 1]
                hred[...] = own
                hfull[h_rows(gme), :] = own
                start(hag)

            @pl.when(t >= LAG)
            def _():
                u = t - LAG
                d = far(u % n_z)
                across(u).wait_recv()

                @pl.when(u < n_z)
                def _():
                    ypart[d] = ypart[d] + oslots[u]
                    over_y(d, 0).start()

                @pl.when(u >= n_z)
                def _():
                    zpart[d] = zpart[d] + oslots[u]

                @pl.when(u == n_z - 1)
                def _():
                    start([over_y(far(v), 1) for v in range(n_z)])
            return carry
        with jax.named_scope("moments"):
            lax.fori_loop(0, 2 * n_z + LAG, moments, 0)

        def forward(t, carry):
            d, h = far(t % n_z), t // n_z
            part = pl.ds(pl.multiple_of(h * rh, rh), rh)
            with jax.named_scope("ywait"):
                over_y(d, h).wait_recv()
            zpart[d, part, :] = zpart[d, part, :] + yslots[d, part, :]

            @pl.when(d > 0)
            def _():
                over_z(d, h).start()
            return carry
        lax.fori_loop(0, n_z, forward, 0)
        with jax.named_scope("hag"):
            finish(hfull.at[pl.ds(0, rank - hw)], h_send.at[1], h_recv.at[1])
        hfull[...] = hfull[...] + eye
        steps = rank // PIVOTS
        per = steps // n_z

        def sweep_forward(t, carry):
            sweep(hfull, t * per, per)
            return forward(n_z + t, carry)
        lax.fori_loop(0, n_z, sweep_forward, 0)
        sweep(hfull, per * n_z, steps - per * n_z)

        def modes_half(z, which, h):
            return m_out.at[pl.ds(pl.multiple_of((z * 2 + which) * rw + h * rh, rh), rh)]

        def gather(d, h):
            ref = modes_half(sz, sy, h)
            return zcopy(1, d, h, ref, ref)

        def pass_on(d, h):
            ref = modes_half(z_from(d), sy, h)
            return ycopy(1, d, h, ref, ref)

        def solve(h, carry):
            with jax.named_scope("zwait"):
                for d in range(1, n_z):
                    over_z(d, h).wait_recv()
            part = pl.ds(pl.multiple_of(h * rh, rh), rh)
            share = zpart[0, part, :]
            for d in range(1, n_z):
                share = share + zslots[d - 1, part, :]
            step = jnp.dot(share, hfull[...], preferred_element_type=F32, precision=lax.Precision.HIGHEST)
            mine = pl.ds(pl.multiple_of(sme * rw + h * rh, rh), rh)
            m_out[mine, :] = m_out[mine, :] - step
            start([gather(far(t), h) for t in range(n_z - 1)])
            pass_on(0, h).start()
            return carry
        lax.fori_loop(0, 2, solve, 0)

        def near(u):
            return jnp.where(u == 0, 1, n_z - u)

        def block_of(i):
            u = i % n_z
            d = jnp.where(u == 0, 0, near(u - 1))
            return d, row_block(z_from(d), jnp.where(i < n_z, sy, 1 - sy))

        def hand_over(i):
            part = pl.ds(pl.multiple_of(block_of(i)[1], rw), rw)
            return ccopy(1, i, m_out.at[part], m_far.at[part])

        def take(ref, which, i):
            block = block_of(i)[1]
            part = pl.ds(pl.multiple_of(which * rows + block, rw), rw)
            prepare_rows(part, ref[pl.ds(pl.multiple_of(block, rw), rw), :])
            error_rows(part)

        def take_own(i):
            @pl.when(more)
            def _():
                hand_over(i).start()
                take(m_out, core, i)

        def take_far(i):
            @pl.when(more)
            def _():
                with jax.named_scope("farwait"):
                    hand_over(i).wait_recv()
                take(m_far, 1 - core, i)
        take_own(0)

        def first_half(u, carry):
            with jax.named_scope("gatherz"):
                gather(near(u), 0).wait_recv()
            pass_on(near(u), 0).start()
            return carry
        lax.fori_loop(0, n_z - 1, first_half, 0)

        def second_half(u, carry):
            with jax.named_scope("gatherz"):
                gather(near(u), 1).wait_recv()
            pass_on(near(u), 1).start()
            take_own(1 + u)
            return carry
        lax.fori_loop(0, n_z - 1, second_half, 0)

        def other(u, carry):
            take_far(u)
            d = block_of(u)[0]
            with jax.named_scope("gathery"):
                pass_on(d, 0).wait_recv()
                pass_on(d, 1).wait_recv()
            take_own(n_z + u)
            return carry
        with jax.named_scope("other"):
            lax.fori_loop(0, n_z, other, 0)

        def last(u, carry):
            take_far(n_z + u)
            return carry
        lax.fori_loop(0, n_z, last, 0)

        @pl.when(more)
        def _():
            send_limit(0)
            gram_part()
            sent(m_out, c_send.at[1], c_recv.at[1, 0])
        with jax.named_scope("sends"):
            sent(opart, c_send.at[0], c_recv.at[0, 0])
            sent(ypart, y_send.at[0], y_recv.at[0, 0, 0])
            sent(m_out.at[pl.ds(0, n_z * rw)], y_send.at[1], y_recv.at[1, 0, 0])
            sent(zslots, z_send.at[0], z_recv.at[0, 0, 0])
            sent(m_out.at[pl.ds(0, (n_z - 1) * rw)], z_send.at[1], z_recv.at[1, 0, 0])
        return carry
    lax.fori_loop(0, OUTER, outer, 0)
    amplitudes.wait_recv()
    amplitudes.wait_send()


def write_out(modes, amplitudes, m_hbm, a_hbm, sem):
    copies = [pltpu.make_async_copy(modes, m_hbm, sem.at[0]), pltpu.make_async_copy(amplitudes, a_hbm, sem.at[1])]
    for copy in copies:
        copy.start()
    for copy in copies:
        copy.wait()


def shards(n_pts, n_snap, snapshots, modes_init, coefs_init):
    rows, width = snapshots.shape
    rank = modes_init.shape[1]
    rw, half, group = rows // n_snap, width // 2, 2 * n_snap
    chunks, n_x, n_z, n_dev = half // CHUNK, n_pts // 2, n_snap // 2, n_pts * n_snap
    hw = rank // group
    vmem, dma = pltpu.VMEM, pltpu.SemaphoreType.DMA
    scratch = [
        vmem((2 * rows, half), F32), vmem((2 * rows, half), F32), vmem((rows, half), F32), vmem((rows, half), F32),
        vmem((rows, rank), F32), vmem((rank, half), F32), vmem((rank, half), F32),
        vmem((2 * rows, 2 * rank), BF16), vmem((2 * rank, 2 * rows), BF16),
        vmem((2 * rank, half), BF16), vmem((2 * rank, half), BF16), vmem((half, 2 * rank), BF16),
        vmem((8, STEP), F32),
        vmem((n_x, rank, rank), F32), vmem((rank, rank), F32),
        vmem((rank, rank), F32), vmem((group - 1, hw, rank), F32), vmem((hw, rank), F32), vmem((rank, rank), F32),
        vmem((INNER + 1, n_dev, 128), F32),
        vmem((INNER, n_x, chunks, rank, CHUNK), F32),
        vmem((n_snap, rw, rank), F32), vmem((n_snap, rw, rank), F32),
        vmem((n_z, rw, rank), F32), vmem((n_z, rw, rank), F32),
        vmem((n_z, rw, rank), F32), vmem((n_z - 1, rw, rank), F32),
        dma((3 + width // STEP,)),
        dma, dma((n_x - 1,)),
        dma((2,)), dma((2,)),
        dma((6,)), dma((4, n_snap)),
        dma, dma((chunks, n_x - 1)),
        dma((INNER + 1,)), dma((INNER + 1,)),
        dma((2,)), dma((2, n_z, 2)),
        dma((2,)), dma((2, n_z - 1, 2)),
    ]
    modes, coefs = pl.pallas_call(
        functools.partial(kernel, n_pts, n_snap),
        out_shape=(vmem((rows, rank), F32), vmem((rank, width), F32)),
        in_specs=[pl.BlockSpec(memory_space=pltpu.HBM)] * 3,
        out_specs=(pl.BlockSpec(memory_space=vmem), pl.BlockSpec(memory_space=vmem)),
        scratch_shapes=scratch,
        compiler_params=pltpu.CompilerParams(collective_id=0, has_side_effects=True, vmem_limit_bytes=67043328 - 5 * 256 * 1024),
    )(snapshots, modes_init, coefs_init)
    return pl.pallas_call(
        write_out,
        out_shape=(jax.ShapeDtypeStruct((rows, rank), F32), jax.ShapeDtypeStruct((rank, width), F32)),
        in_specs=[pl.BlockSpec(memory_space=pl.ANY)] * 2,
        out_specs=(pl.BlockSpec(memory_space=pltpu.HBM), pl.BlockSpec(memory_space=pltpu.HBM)),
        scratch_shapes=[dma((2,))],
    )(pltpu.with_memory_space_constraint(modes, vmem), pltpu.with_memory_space_constraint(coefs, vmem))


def solution(mesh):
    in_specs = (P("pts", "snap"), P("pts", None), P(None, "snap"))
    out_specs = (P("pts", None), P(None, "snap"))
    body = functools.partial(shards, mesh.shape["pts"], mesh.shape["snap"])
    return jax.shard_map(body, mesh=mesh, in_specs=in_specs, out_specs=out_specs, check_vma=False)
```

time: 119 us -> 116 us (0.975)
  Pallas kernels: 118 us -> 115 us
    pallas_call x1, Pallas kernels: 117 us -> 114 us  [shards(): pl.pallas_call(functools.partial(kernel, n_pts, n_snap), out_shape=(vmem(...]
where the time goes in v7:
time: 116 us
  Pallas kernels  115 us (99%)
    pallas_call x1, Pallas kernels, shards(): pl.pallas_call(functools.partial(kernel, n_pts, n_snap), out_shape=(vmem(...  114 us

profile of v7, /device:TPU:0, one launch (start us, length us, event | category | flops | bytes accessed | tf_op | source)
XLA Modules:
  0.0 115.6 jit_solution(16285218443935234845)
XLA Ops:
  0.6 114.0 %shard_map.50 = (f32[1024,128]{1,0:T(8,128)S(1)}, f32[128,1024]{1,0:T(8,128)S(1)}) custom-call(f32[1024,1024]{1,0:T(8,128)} %s_hbm.1, f32[1024,128]{1,0:T(8,128)} %m_hbm.1, f32[128,1024]{1,0:T(8,128)} %c_hbm.1), custom_call_target="tpu_custom_call" | custom-call | tf_op jit(solution)/shard_map/pallas_call | solution.py:626
  114.6 1.0 shard_map.51

commit v8 on v7

--- a/solution.py
+++ b/solution.py
@@ -12,7 +12,7 @@
 PIVOTS = 16
 CHUNK = 128
 STEP = 256
-LAG = 2
+LAG = 3
 
 HUBER = 1.345
 RIDGE = 0.01
@@ -550,24 +550,22 @@
                 gather(near(u), 1).wait_recv()
             pass_on(near(u), 1).start()
             take_own(1 + u)
+            take_far(u)
             return carry
         lax.fori_loop(0, n_z - 1, second_half, 0)
 
         def other(u, carry):
-            take_far(u)
             d = block_of(u)[0]
             with jax.named_scope("gathery"):
                 pass_on(d, 0).wait_recv()
                 pass_on(d, 1).wait_recv()
             take_own(n_z + u)
+            take_far(n_z + u - 1)
             return carry
         with jax.named_scope("other"):
             lax.fori_loop(0, n_z, other, 0)
 
-        def last(u, carry):
-            take_far(n_z + u)
-            return carry
-        lax.fori_loop(0, n_z, last, 0)
+        take_far(2 * n_z - 1)
 
         @pl.when(more)
         def _():

time: 116 us -> 115 us (level)
  no operation moved by 1% of the time
where the time goes in v8:
time: 115 us
  Pallas kernels  114 us (99%)
    pallas_call x1, Pallas kernels, shards(): pl.pallas_call(functools.partial(kernel, n_pts, n_snap), out_shape=(vmem(...  113 us

profile of v8, /device:TPU:0, one launch (start us, length us, event | category | flops | bytes accessed | tf_op | source)
XLA Modules:
  0.0 114.9 jit_solution(13850577768170108408)
XLA Ops:
  0.6 113.3 %shard_map.50 = (f32[1024,128]{1,0:T(8,128)S(1)}, f32[128,1024]{1,0:T(8,128)S(1)}) custom-call(f32[1024,1024]{1,0:T(8,128)} %s_hbm.1, f32[1024,128]{1,0:T(8,128)} %m_hbm.1, f32[128,1024]{1,0:T(8,128)} %c_hbm.1), custom_call_target="tpu_custom_call" | custom-call | tf_op jit(solution)/shard_map/pallas_call | solution.py:624
  113.9 1.0 shard_map.51

commit v9 on v8

--- a/solution.py
+++ b/solution.py
@@ -49,7 +49,7 @@
            s, e, s_far, e_far, m_far, c_now, c_far, mcat, mtcat, ccat, ccat_far, ctcat, sq,
            gslots, gfull, hpart, hslots, hred, hfull,
            lslots, xslots, opart, oslots, ypart, yslots, zpart, zslots,
-           load_sem, g_send, g_recv, h_send, h_recv, c_send, c_recv, x_send, x_recv,
+           load_sem, g_send, g_recv, h_send, h_recv, c_send, c_recv, once, x_send, x_recv,
            l_send, l_recv, y_send, y_recv, z_send, z_recv):
     rows, rank = m_out.shape
     width = c_out.shape[1]
@@ -128,7 +128,8 @@
 
     def ccopy(site, k, src, dst):
         return pltpu.make_async_remote_copy(
-            src_ref=src, dst_ref=dst, send_sem=c_send.at[site + k if site == 2 else site], recv_sem=c_recv.at[min(site, 3), k],
+            src_ref=src, dst_ref=dst, send_sem=c_send.at[site + k if site == 2 else site],
+            recv_sem=c_recv.at[site, k] if site < 2 else once.at[k + site - 2],
             device_id={"pts": px * 2 + 1 - core}, device_id_type=MESH)
 
     def xcopy(site, k, d):
@@ -348,9 +349,9 @@
                 def _():
                     with jax.named_scope("sswap"):
                         swap[2].wait_recv()
-                    sent(m_out, c_send.at[2], c_recv.at[2, 0])
-                    sent(e_far, c_send.at[3], c_recv.at[2, 1])
-                    sent(s_far, c_send.at[4], c_recv.at[2, 2])
+                    sent(m_out, c_send.at[2], once.at[0])
+                    sent(e_far, c_send.at[3], once.at[1])
+                    sent(s_far, c_send.at[4], once.at[2])
             wide = CHUNK
 
             def update(j, carry):
@@ -615,7 +616,7 @@
         dma((3 + width // STEP,)),
         dma, dma((n_x - 1,)),
         dma((2,)), dma((2,)),
-        dma((6,)), dma((4, n_snap)),
+        dma((6,)), dma((2, n_snap)), dma((4,)),
         dma, dma((chunks, n_x - 1)),
         dma((INNER + 1,)), dma((INNER + 1,)),
         dma((2,)), dma((2, n_z, 2)),

time: 115 us -> 115 us (level)
  no operation moved by 1% of the time
where the time goes in v9:
time: 115 us
  Pallas kernels  114 us (99%)
    pallas_call x1, Pallas kernels, shards(): pl.pallas_call(functools.partial(kernel, n_pts, n_snap), out_shape=(vmem(...  113 us

profile of v9, /device:TPU:0, one launch (start us, length us, event | category | flops | bytes accessed | tf_op | source)
XLA Modules:
  0.0 114.8 jit_solution(15459854424799029349)
XLA Ops:
  0.6 113.2 %shard_map.50 = (f32[1024,128]{1,0:T(8,128)S(1)}, f32[128,1024]{1,0:T(8,128)S(1)}) custom-call(f32[1024,1024]{1,0:T(8,128)} %s_hbm.1, f32[1024,128]{1,0:T(8,128)} %m_hbm.1, f32[128,1024]{1,0:T(8,128)} %c_hbm.1), custom_call_target="tpu_custom_call" | custom-call | tf_op jit(solution)/shard_map/pallas_call | solution.py:625
  113.8 1.0 shard_map.51

commit v10 on v9

--- a/solution.py
+++ b/solution.py
@@ -47,7 +47,7 @@
 
 def kernel(n_pts, n_snap, s_hbm, m_hbm, c_hbm, m_out, c_out,
            s, e, s_far, e_far, m_far, c_now, c_far, mcat, mtcat, ccat, ccat_far, ctcat, sq,
-           gslots, gfull, hpart, hslots, hred, hfull,
+           gslots, gfull, gcat, hpart, hslots, hred, hfull, hcat,
            lslots, xslots, opart, oslots, ypart, yslots, zpart, zslots,
            load_sem, g_send, g_recv, h_send, h_recv, c_send, c_recv, once, x_send, x_recv,
            l_send, l_recv, y_send, y_recv, z_send, z_recv):
@@ -344,6 +344,8 @@
                 gfull[...] = total + eye
                 sent(gslots.at[pl.ds(0, n_x - 1)], g_send, g_recv.at[0])
                 sweep(gfull, 0, rank // PIVOTS)
+                h, m, l = split3(gfull[...])
+                gcat[...] = jnp.concatenate([h, h, m, h, m, l], 1)
 
                 @pl.when(o == 0)
                 def _():
@@ -363,7 +365,8 @@
                     share = xslots[inner, 0, k]
                     for x in range(1, n_x):
                         share = share + xslots[inner, x, k]
-                    step = jnp.dot(gfull[...], share, preferred_element_type=F32, precision=lax.Precision.HIGHEST)
+                    h, m, l = split3(share)
+                    step = dot(gcat[...], jnp.concatenate([h, m, h, l, m, h], 0))
                     cols = pl.ds(pl.multiple_of(k * CHUNK, CHUNK), CHUNK)
                     value = c_now[:, cols] - step
                     c_now[:, cols] = value
@@ -480,6 +483,9 @@
         lax.fori_loop(0, n_z, sweep_forward, 0)
         sweep(hfull, per * n_z, steps - per * n_z)
 
+        a3, b3, c3 = split3(hfull[...])
+        hcat[...] = jnp.concatenate([a3, b3, a3, c3, b3, a3], 0)
+
         def modes_half(z, which, h):
             return m_out.at[pl.ds(pl.multiple_of((z * 2 + which) * rw + h * rh, rh), rh)]
 
@@ -499,7 +505,8 @@
             share = zpart[0, part, :]
             for d in range(1, n_z):
                 share = share + zslots[d - 1, part, :]
-            step = jnp.dot(share, hfull[...], preferred_element_type=F32, precision=lax.Precision.HIGHEST)
+            h3, m3, l3 = split3(share)
+            step = dot(jnp.concatenate([h3, h3, m3, h3, m3, l3], 1), hcat[...])
             mine = pl.ds(pl.multiple_of(sme * rw + h * rh, rh), rh)
             m_out[mine, :] = m_out[mine, :] - step
             start([gather(far(t), h) for t in range(n_z - 1)])
@@ -606,8 +613,9 @@
         vmem((2 * rows, 2 * rank), BF16), vmem((2 * rank, 2 * rows), BF16),
         vmem((2 * rank, half), BF16), vmem((2 * rank, half), BF16), vmem((half, 2 * rank), BF16),
         vmem((8, STEP), F32),
-        vmem((n_x, rank, rank), F32), vmem((rank, rank), F32),
+        vmem((n_x, rank, rank), F32), vmem((rank, rank), F32), vmem((rank, 6 * rank), BF16),
         vmem((rank, rank), F32), vmem((group - 1, hw, rank), F32), vmem((hw, rank), F32), vmem((rank, rank), F32),
+        vmem((6 * rank, rank), BF16),
         vmem((INNER + 1, n_dev, 128), F32),
         vmem((INNER, n_x, chunks, rank, CHUNK), F32),
         vmem((n_snap, rw, rank), F32), vmem((n_snap, rw, rank), F32),

time: 115 us -> 115 us (level)
  no operation moved by 1% of the time
where the time goes in v10:
time: 115 us
  Pallas kernels  114 us (99%)
    pallas_call x1, Pallas kernels, shards(): pl.pallas_call(functools.partial(kernel, n_pts, n_snap), out_shape=(vmem(...  113 us

profile of v10, /device:TPU:0, one launch (start us, length us, event | category | flops | bytes accessed | tf_op | source)
XLA Modules:
  0.0 114.9 jit_solution(1382499897930642559)
XLA Ops:
  0.6 113.3 %shard_map.50 = (f32[1024,128]{1,0:T(8,128)S(1)}, f32[128,1024]{1,0:T(8,128)S(1)}) custom-call(f32[1024,1024]{1,0:T(8,128)} %s_hbm.1, f32[1024,128]{1,0:T(8,128)} %m_hbm.1, f32[128,1024]{1,0:T(8,128)} %c_hbm.1), custom_call_target="tpu_custom_call" | custom-call | tf_op jit(solution)/shard_map/pallas_call | solution.py:633
  114.0 1.0 shard_map.51

commit v11 on v9

--- a/solution.py
+++ b/solution.py
@@ -84,10 +84,6 @@
     others = [(dx, dc, dz, dy) for dx in range(n_x) for dc in range(2) for dz in range(n_z) for dy in range(2)][1:]
     others.sort(key=lambda d: -hops(d))
 
-    barrier = pltpu.get_barrier_semaphore()
-    for d in others:
-        pl.semaphore_signal(barrier, inc=1, device_id=offset(d), device_id_type=MESH)
-
     def step_cols(j):
         return pl.ds(pl.multiple_of(j * STEP, STEP), STEP)
 
@@ -110,6 +106,10 @@
     start_all = [load_m, load_c] + [load_own(j) for j in range(loads)] + [load_c_far] + [load_far(j) for j in range(loads)]
     for copy in start_all:
         copy.start()
+
+    barrier = pltpu.get_barrier_semaphore()
+    for d in others:
+        pl.semaphore_signal(barrier, inc=1, device_id=offset(d), device_id_type=MESH)
 
     def gcopy(d):
         ref = gslots.at[px]

time: 115 us -> 115 us (level)
  no operation moved by 1% of the time
where the time goes in v11:
time: 115 us; the launch traced here: 114 us
  Pallas kernels  114 us (99%)
    pallas_call x1, Pallas kernels, shards(): pl.pallas_call(functools.partial(kernel, n_pts, n_snap), out_shape=(vmem(...  113 us

profile of v11, /device:TPU:0, one launch (start us, length us, event | category | flops | bytes accessed | tf_op | source)
XLA Modules:
  0.0 114.5 jit_solution(2769700604491276546)
XLA Ops:
  0.6 112.9 %shard_map.50 = (f32[1024,128]{1,0:T(8,128)S(1)}, f32[128,1024]{1,0:T(8,128)S(1)}) custom-call(f32[1024,1024]{1,0:T(8,128)} %s_hbm.1, f32[1024,128]{1,0:T(8,128)} %m_hbm.1, f32[128,1024]{1,0:T(8,128)} %c_hbm.1), custom_call_target="tpu_custom_call" | custom-call | tf_op jit(solution)/shard_map/pallas_call | solution.py:625
  113.5 1.0 shard_map.51

commit v12 on v11

--- a/solution.py
+++ b/solution.py
@@ -103,7 +103,7 @@
     load_m = pltpu.make_async_copy(m_hbm, m_out, load_sem.at[0])
     load_c = pltpu.make_async_copy(c_hbm.at[:, side(core)], c_now, load_sem.at[1])
     load_c_far = pltpu.make_async_copy(c_hbm.at[:, side(1 - core)], c_far, load_sem.at[2])
-    start_all = [load_m, load_c] + [load_own(j) for j in range(loads)] + [load_c_far] + [load_far(j) for j in range(loads)]
+    start_all = [load_m, load_c, load_own(0), load_c_far] + [load_own(j) for j in range(1, loads)] + [load_far(j) for j in range(loads)]
     for copy in start_all:
         copy.start()
 

time: 115 us -> 115 us (level)
  no operation moved by 1% of the time
where the time goes in v12:
time: 115 us
  Pallas kernels  114 us (99%)
    pallas_call x1, Pallas kernels, shards(): pl.pallas_call(functools.partial(kernel, n_pts, n_snap), out_shape=(vmem(...  113 us

profile of v12, /device:TPU:0, one launch (start us, length us, event | category | flops | bytes accessed | tf_op | source)
XLA Modules:
  0.0 114.5 jit_solution(6506140438002834250)
XLA Ops:
  0.6 112.9 %shard_map.50 = (f32[1024,128]{1,0:T(8,128)S(1)}, f32[128,1024]{1,0:T(8,128)S(1)}) custom-call(f32[1024,1024]{1,0:T(8,128)} %s_hbm.1, f32[1024,128]{1,0:T(8,128)} %m_hbm.1, f32[128,1024]{1,0:T(8,128)} %c_hbm.1), custom_call_target="tpu_custom_call" | custom-call | tf_op jit(solution)/shard_map/pallas_call | solution.py:625
  113.5 1.0 shard_map.51
